TPU v7x, 256 devices: a whole 4x4x8 slice. The times are simulated.
256 devices in a mesh: tile: 32 (over z_hi, x, core), grp: 8 (over z_lo, y).
Axes of the slice: x: 4, y: 4, z: 8 (z_hi: 4, z_lo: 2; z = z_hi * 2 + z_lo), core: 2. Of those that a mesh axis runs over, the one named last changes fastest.
Arguments:
- traces: float32 [1024, 16, 1500], P(('tile', 'grp')), may hold values from -6 to 6
- validity: int32 [1024, 16], P(('tile', 'grp')), may hold values 0 or 1
- boundary_rows: int32 [256, 2, 4], P(('tile', 'grp')), may hold values from 0 to 3, as said below
- boundary_count: int32 [256, 2], P(('tile', 'grp')), may hold values from 1 to 4, as said below
- pair_mask: int32 [1024, 96], P(('tile', 'grp')), may hold values from 0 to 1, as said below
Outputs:
- correlations: bfloat16 [1024, 96, 2001], P(('tile', 'grp'))
Inputs may be any that keep to these rules, and one draw needn't show every extreme that they name: `boundary_rows`: each device's list in each direction orders all of its 4 local stations, each once. `boundary_count`: in every draw some device sends all 4 of its stations in each direction. `pair_mask`: a station's column for itself is 0.
All inputs are finite; a program needn't handle non-finite values. No bound on the sum of `validity` on one device may be relied on, other than what follows from the above.
Results may differ from a plain program's by a relative error of at most 0.008.
Values may be sent and summed in bfloat16 or wider, within the bound.
A program may use at most 64 MiB of HBM per device.

v0:
```python
import math

import jax
import jax.numpy as jnp
from jax import lax
from jax.sharding import PartitionSpec as P

SAMP = 1500
NBIN = 144
MAXLAG = 1000
LAGS = 2001


def passed_along(array, axis, by):
    count = lax.axis_size(axis)
    pairs = [(i, i + by) for i in range(count) if 0 <= i + by < count]
    return lax.ppermute(array, axis, pairs)


def fourier_table(samples):
    points = 2 * samples
    sample_number = jnp.arange(samples, dtype=jnp.int32)[:, None]
    freq_number = jnp.arange(1, NBIN + 1, dtype=jnp.int32)[None, :]
    angles = jnp.mod(sample_number * freq_number, points).astype(jnp.float32) * (
        2.0 * jnp.pi / points
    )
    return jnp.concatenate([jnp.cos(angles), -jnp.sin(angles)], axis=1)


def lag_basis():
    points = 2 * SAMP
    freq_number = jnp.arange(1, NBIN + 1, dtype=jnp.int32)[:, None]
    lag_number = jnp.arange(LAGS, dtype=jnp.int32)[None, :] - MAXLAG
    angles = jnp.mod(freq_number * lag_number, points).astype(jnp.float32) * (2.0 * jnp.pi / points)
    return jnp.concatenate([jnp.cos(angles), -jnp.sin(angles)], axis=0)


def whitened(traces, valid_float):
    stations, segments, samples = traces.shape
    sample_number = jnp.arange(samples, dtype=jnp.float32)
    hann_taper = 0.5 - 0.5 * jnp.cos(sample_number * (2.0 * jnp.pi / samples))
    flat_traces = (traces * hann_taper).reshape(stations * segments, samples)
    spectrum = jnp.dot(
        flat_traces,
        fourier_table(samples),
        precision=lax.Precision.HIGHEST,
        preferred_element_type=jnp.float32,
    )
    spectrum = spectrum.reshape(stations, segments, 2, NBIN)
    real_part = spectrum[:, :, 0]
    imag_part = spectrum[:, :, 1]
    power_bins = real_part * real_part + imag_part * imag_part
    padded = jnp.pad(power_bins, ((0, 0), (0, 0), (4, 4)))
    smooth = sum((padded[:, :, offset : offset + NBIN] for offset in range(9))) / 9.0
    mean_power = jnp.mean(power_bins, axis=2, keepdims=True)
    factor = valid_float[:, :, None] / jnp.sqrt(0.5 * smooth + 0.5 * mean_power + 1e-06)
    return jnp.stack([real_part * factor, imag_part * factor], axis=2).astype(jnp.bfloat16)


def stacked(left_spec, left_mask, right_spec, right_mask):
    left_both = jnp.concatenate([left_spec[:, :, 0], left_spec[:, :, 1]], axis=1)
    right_real = right_spec[:, :, 0]
    right_imag = right_spec[:, :, 1]
    right_both = jnp.stack(
        [
            jnp.concatenate([right_real, right_imag], axis=1),
            jnp.concatenate([-right_imag, right_real], axis=1),
        ],
        axis=1,
    )
    product = jnp.einsum(
        "iqf,jcqf->ijcf", left_both, right_both, preferred_element_type=jnp.float32
    )
    pair_count = jnp.einsum("iq,jq->ij", left_mask, right_mask, preferred_element_type=jnp.float32)
    return (product / jnp.maximum(pair_count, 1.0)[:, :, None, None]).astype(jnp.bfloat16)


def on_device(traces, validity, boundary_rows, boundary_count, pair_mask):
    per_device = traces.shape[0]
    valid_float = validity.astype(jnp.float32)
    valid_half = validity.astype(jnp.bfloat16)
    own_spec = whitened(traces, valid_float)
    slot_number = jnp.arange(per_device, dtype=jnp.int32)
    live_up = (slot_number < boundary_count[0, 0]).astype(jnp.float32)
    live_down = (slot_number < boundary_count[0, 1]).astype(jnp.float32)
    picks_up = boundary_rows[0, 0]
    picks_down = boundary_rows[0, 1]
    below_traces, below_mask = passed_along(
        (
            jnp.take(traces, picks_up, axis=0) * live_up[:, None, None],
            jnp.take(valid_float, picks_up, axis=0) * live_up[:, None],
        ),
        "tile",
        1,
    )
    above_traces, above_mask = passed_along(
        (
            jnp.take(traces, picks_down, axis=0) * live_down[:, None, None],
            jnp.take(valid_float, picks_down, axis=0) * live_down[:, None],
        ),
        "tile",
        -1,
    )
    recv_spec = whitened(
        jnp.concatenate([below_traces, above_traces], axis=0),
        jnp.concatenate([below_mask, above_mask], axis=0),
    )
    recv_mask = jnp.concatenate([below_mask, above_mask], axis=0).astype(jnp.bfloat16)
    local_spec = jnp.concatenate([own_spec, recv_spec], axis=0)
    local_mask = jnp.concatenate([valid_half, recv_mask], axis=0)
    all_spec, all_mask = (
        lax.all_gather(local_spec, "grp", axis=0, tiled=True),
        lax.all_gather(local_mask, "grp", axis=0, tiled=True),
    )
    cross_spec = stacked(own_spec, valid_half, all_spec, all_mask)
    columns = cross_spec.shape[1]
    basis = lag_basis()
    basis_high = basis.astype(jnp.bfloat16)
    basis_low = (basis - basis_high.astype(jnp.float32)).astype(jnp.bfloat16)
    flat_cross = cross_spec.reshape(per_device * columns, 2 * NBIN)
    series = jnp.dot(flat_cross, basis_high, preferred_element_type=jnp.float32)
    series = series + jnp.dot(flat_cross, basis_low, preferred_element_type=jnp.float32)
    series = series.reshape(per_device, columns, -1)
    scaled = series * (pair_mask.astype(jnp.float32) / math.sqrt(NBIN))[:, :, None]
    return scaled.astype(jnp.bfloat16)


def solution(mesh):
    return jax.shard_map(
        on_device,
        mesh=mesh,
        in_specs=(
            P(("tile", "grp"), None, None),
            P(("tile", "grp"), None),
            P(("tile", "grp"), None, None),
            P(("tile", "grp"), None),
            P(("tile", "grp"), None),
        ),
        out_specs=P(("tile", "grp"), None, None),
        check_vma=False,
    )
```

profile of v0, /device:TPU:64, one launch (start us, length us, event | category | flops | bytes accessed | tf_op | source)
XLA Modules:
  0.0 116.2 jit_solution(16800844627624242405)
XLA Ops:
  0.0 1.3 %fusion.42 = (s32[1,1]{1,0:T(1,128)}, s32[1,1]{1,0:T(1,128)}) fusion(s32[1,2]{1,0:T(1,128)} %param.12), kind=kLoop, calls=%fused_computation.103 | loop fusion | bytes 16 | tf_op jit(solution)/shard_map/slice | solution.py:84
  1.3 1.4 %compare_and_fusion.1 = (pred[4]{0:T(512)(128)(4,1)S(1)}, s32[4]{0:T(128)S(1)}, pred[4]{0:T(512)(128)(4,1)S(1)}, s32[4]{0:T(128)S(1)}, f32[4]{0:T(128)S(1)}) fusion(s32[1,2,4]{2,1,0:T(2,128)} %param.11, s32[]{:T(128)} %bitcast.12), kind=kLoop, calls=%fused_computation.90 | loop fusion | flops 56 | bytes 92 | tf_op jit(solution)/shard_map/jit(_take)/and | solution.py:90
  2.7 0.0 copy-start.5
  2.8 1.6 %gather_fusion.1 = f32[4,16,1500]{2,1,0:T(8,128)S(1)} fusion(f32[4,16,1500]{2,1,0:T(8,128)} %param.9, s32[1024]{0:T(1024)S(1)} %pad_clamp_fusion), kind=kCustom, calls=%fused_computation.2.clone | custom fusion | bytes 768016 | tf_op jit(solution)/shard_map/jit(_take)/gather | solution.py:98
  4.3 0.1 select_multiply_fusion
  4.4 3.2 %collective-permute-start.1 = (f32[4,16,1500]{2,1,0:T(8,128)S(1)}, f32[4,16,1500]{2,1,0:T(8,128)S(1)}, u32[]{:S(2)}, u32[]{:S(2)}) collective-permute-start(f32[4,16,1500]{2,1,0:T(8,128)S(1)} %select_multiply_fusion), channel_id=1, source_target_pairs={{8,0},{16,8},{24,16},{32,24},{40,32},{48,40},{56,48},{64,56},{72,6... | collective-permute-start | bytes 1152008 | tf_op jit(solution)/shard_map/ppermute | solution.py:17
  7.7 0.6 gather_fusion
  8.3 0.7 compare_convert_fusion.1
  8.9 0.1 select_multiply_fusion.1
  9.0 1.9 %collective-permute-start = (f32[4,16,1500]{2,1,0:T(8,128)S(1)}, f32[4,16,1500]{2,1,0:T(8,128)}, u32[]{:S(2)}, u32[]{:S(2)}) collective-permute-start(f32[4,16,1500]{2,1,0:T(8,128)S(1)} %select_multiply_fusion.1), channel_id=1, source_target_pairs={{0,8},{8,16},{16,24},{24,32},{32,40},{40,48},{48,56},{56,64},{64,7... | collective-permute-start | bytes 1152008 | tf_op jit(solution)/shard_map/ppermute | solution.py:17
  11.0 0.6 gather_fusion.3
  11.5 0.1 select_multiply_fusion.2
  11.6 6.6 %collective-permute-start.3 = (f32[4,16]{1,0:T(4,128)S(1)}, f32[4,16]{1,0:T(4,128)S(1)}, u32[]{:S(2)}, u32[]{:S(2)}) collective-permute-start(f32[4,16]{1,0:T(4,128)S(1)} %select_multiply_fusion.2), channel_id=1, source_target_pairs={{8,0},{16,8},{24,16},{32,24},{40,32},{48,40},{56,48},{64,56},{72,6... | collective-permute-start | bytes 776 | tf_op jit(solution)/shard_map/ppermute | solution.py:17
  18.2 0.6 gather_fusion.2
  18.8 0.1 select_multiply_fusion.3
  18.9 1.9 %collective-permute-start.2 = (f32[4,16]{1,0:T(4,128)S(1)}, f32[4,16]{1,0:T(4,128)S(1)}, u32[]{:S(2)}, u32[]{:S(2)}) collective-permute-start(f32[4,16]{1,0:T(4,128)S(1)} %select_multiply_fusion.3), channel_id=1, source_target_pairs={{0,8},{8,16},{16,24},{24,32},{32,40},{40,48},{48,56},{56,64},{64,7... | collective-permute-start | bytes 776 | tf_op jit(solution)/shard_map/ppermute | solution.py:17
  20.8 0.1 multiply_subtract_fusion
  20.9 3.7 %fusion.16 = (f32[1500,144]{0,1:T(8,128)S(1)}, f32[1500,144]{0,1:T(8,128)S(1)}) fusion(s32[144]{0:T(256)S(1)} %iota_add_fusion.1), kind=kLoop, calls=%fused_computation.35 | loop fusion | flops 2160000 | bytes 1728576 | tf_op jit(solution)/shard_map/cos | solution.py:27
  24.5 0.1 pad_maximum_fusion.2
  24.7 1.9 %fusion.23 = f32[4,16,2,144]{3,1,2,0:T(8,128)S(1)} fusion(f32[2,144,1500,1]{2,1,0,3:T(8,128)S(1)} %bitcast.98, f32[4,16,1500]{2,1,0:T(8,128)S(1)} %copy-done.4, f32[1500]{0:T(1024)S(1)} %multiply_subtract_fusion), kind=kOutput, calls=%fused_computation.44 | convolution fusion | flops 331872000 | bytes 2191728 | tf_op jit(solution)/shard_map/dot_general | solution.py:43
  26.6 0.0 copy-start.6
  26.6 0.1 fusion.39
  26.7 0.2 multiply_convert_fusion.4
  27.0 6.1 %fusion.9 = (f32[144,2001]{1,0:T(8,128)}, f32[144,2001]{1,0:T(8,128)}) fusion(s32[2001]{0:T(1024)S(1)} %iota_add_fusion, s32[144]{0:T(256)S(1)} %iota_add_fusion.1), kind=kLoop, calls=%fused_computation.25 | loop fusion | flops 2881440 | bytes 2313732 | tf_op jit(solution)/shard_map/cos | solution.py:35
  33.1 0.2 copy.27
  33.3 0.0 collective-permute-done.2
  33.3 29.0 %all-gather = bf16[8,12,16]{2,1,0:T(8,128)(2,1)S(1)} all-gather(bf16[1,12,16]{2,1,0:T(8,128)(2,1)S(1)} %maximum_bitcast_fusion.3), channel_id=1, replica_groups=mesh['tile'=32,'grp'=8] {'grp'}, dimensions={0}, use_global_device_ids=true | all-gather | bytes 3456 | tf_op jit(solution)/shard_map/all_gather | solution.py:113
  62.4 0.1 fusion.11
  62.5 0.0 collective-permute-done.1
  62.5 0.0 collective-permute-done
  62.5 2.6 %fusion.19 = f32[8,16,2,144]{3,1,2,0:T(8,128)S(1)} fusion(f32[2,144,1500,1]{2,1,0,3:T(8,128)S(1)} %bitcast.99, f32[4,16,1500]{2,1,0:T(8,128)S(1)} %collective-permute-done.1, f32[4,16,1500]{2,1,0:T(8,128)} %collective-permute-done, f32[1500]{0:T(1024)S(1)} %multiply_subtract_fusion), kind=kOutput, calls=%fused_computation.41 | convolution fusion | flops 663936000 | bytes 2649456 | tf_op jit(solution)/shard_map/dot_general | solution.py:43
  65.2 0.1 fusion.40
  65.3 0.4 fusion.30
  65.8 32.0 %all_gather.6 = bf16[96,16,2,144]{3,1,0,2:T(8,128)(2,1)S(1)} all-gather(bf16[12,16,2,144]{3,1,0,2:T(8,128)(2,1)S(1)} %maximum_maximum_fusion), channel_id=1, replica_groups=mesh['tile'=32,'grp'=8] {'grp'}, dimensions={0}, use_global_device_ids=true | all-gather | bytes 995328 | tf_op jit(solution)/shard_map/all_gather | solution.py:112
  97.8 0.1 slice_bitcast_fusion
  97.9 0.1 fusion.38
  97.9 0.7 maximum_bitcast_fusion
  98.6 0.6 pad_maximum_fusion
  99.2 5.5 %copy.20 = bf16[96,2,32,144]{0,2,1,3:T(8,128)(2,1)} copy(bf16[96,2,32,144]{3,2,0,1:T(8,128)(2,1)S(1)} %pad_maximum_fusion) | data formatting | bytes 3538944 | tf_op jit(solution)/shard_map/stack | solution.py:64
  104.8 2.3 %fusion.4 = bf16[4,96,2,144]{1,0,2,3:T(4,128)(2,1)S(1)} fusion(bf16[96,2,32,144]{0,2,1,3:T(8,128)(2,1)} %copy.20, bf16[4,32,144,1]{1,0,3,2:T(4,128)(2,1)S(1)} %copy.27, f32[4,96]{1,0:T(4,128)S(1)} %fusion.11), kind=kOutput, calls=%fused_computation.18 | convolution fusion | flops 7299072 | bytes 2029056 | tf_op jit(solution)/shard_map/iqf,jcqf->ijcf/dot_general | solution.py:71
  107.0 0.1 copy.23
  107.1 0.2 reshape.85
  107.4 0.0 copy-start.1
  107.4 1.3 %fusion.1 = f32[384,2001]{0,1:T(8,128)S(1)} fusion(bf16[384,288]{0,1:T(8,128)(2,1)S(1)} %reshape.85, f32[144,2001]{1,0:T(8,128)S(1)} %copy-done.2, f32[144,2001]{1,0:T(8,128)S(1)} %copy-done), kind=kOutput, calls=%fused_computation.14 | convolution fusion | flops 444894336 | bytes 5599872 | tf_op jit(solution)/shard_map/dot_general | solution.py:121
  108.7 0.3 copy-done.3
  109.0 1.3 %convolution_add_fusion = f32[384,2001]{0,1:T(8,128)S(1)} fusion(f32[384,2001]{0,1:T(8,128)S(1)} %fusion.1, bf16[384,288]{0,1:T(8,128)(2,1)S(1)} %reshape.85, f32[144,2001]{1,0:T(8,128)S(1)} %copy-done.3, f32[144,2001]{1,0:T(8,128)S(1)} %copy-done.1), kind=kOutput, calls=%fused_computation.6 | convolution fusion | flops 446239008 | bytes 8673408 | tf_op jit(solution)/shard_map/dot_general | solution.py:122
  110.3 2.6 %copy.24 = f32[384,2001]{1,0:T(8,128)} copy(f32[384,2001]{0,1:T(8,128)S(1)} %convolution_add_fusion) | data formatting | bytes 6147072 | tf_op jit(solution)/shard_map/add | solution.py:122
  112.9 3.3 %multiply_convert_fusion = bf16[4,96,2001]{2,1,0:T(8,128)(2,1)} fusion(f32[4,96,2001]{2,1,0:T(8,128)} %bitcast.100, f32[4,96]{1,0:T(4,128)S(1)} %convert_multiply_fusion), kind=kLoop, calls=%fused_computation.5 | loop fusion | flops 1536768 | bytes 4611840 | tf_op jit(solution)/shard_map/convert_element_type | solution.py:125
  (27 shorter events, 0.2 us)
Async XLA Ops:
  0.0 7.7 %copy-start.4 = (f32[4,16,1500]{2,1,0:T(8,128)S(1)}, f32[4,16,1500]{2,1,0:T(8,128)}, u32[]{:S(2)}) copy-start(f32[4,16,1500]{2,1,0:T(8,128)} %param.9) | copy-start | bytes 1152004
  2.7 8.2 %copy-start.5 = (s32[4,16]{1,0:T(4,128)S(1)}, s32[4,16]{1,0:T(4,128)}, u32[]{:S(2)}) copy-start(s32[4,16]{1,0:T(4,128)} %param.10) | copy-start | bytes 772
  4.4 58.1 %collective-permute-start.1 = (f32[4,16,1500]{2,1,0:T(8,128)S(1)}, f32[4,16,1500]{2,1,0:T(8,128)S(1)}, u32[]{:S(2)}, u32[]{:S(2)}) collective-permute-start(f32[4,16,1500]{2,1,0:T(8,128)S(1)} %select_multiply_fusion), channel_id=1, source_target_pairs={{8,0},{16,8},{24,16},{32,24},{40,32},{48,40},{56,48},{64,56},{72,6... | collective-permute-start | bytes 1152008 | tf_op jit(solution)/shard_map/ppermute | solution.py:17
  9.0 53.5 %collective-permute-start = (f32[4,16,1500]{2,1,0:T(8,128)S(1)}, f32[4,16,1500]{2,1,0:T(8,128)}, u32[]{:S(2)}, u32[]{:S(2)}) collective-permute-start(f32[4,16,1500]{2,1,0:T(8,128)S(1)} %select_multiply_fusion.1), channel_id=1, source_target_pairs={{0,8},{8,16},{16,24},{24,32},{32,40},{40,48},{48,56},{56,64},{64,7... | collective-permute-start | bytes 1152008 | tf_op jit(solution)/shard_map/ppermute | solution.py:17
  11.6 21.7 %collective-permute-start.3 = (f32[4,16]{1,0:T(4,128)S(1)}, f32[4,16]{1,0:T(4,128)S(1)}, u32[]{:S(2)}, u32[]{:S(2)}) collective-permute-start(f32[4,16]{1,0:T(4,128)S(1)} %select_multiply_fusion.2), channel_id=1, source_target_pairs={{8,0},{16,8},{24,16},{32,24},{40,32},{48,40},{56,48},{64,56},{72,6... | collective-permute-start | bytes 776 | tf_op jit(solution)/shard_map/ppermute | solution.py:17
  18.9 14.4 %collective-permute-start.2 = (f32[4,16]{1,0:T(4,128)S(1)}, f32[4,16]{1,0:T(4,128)S(1)}, u32[]{:S(2)}, u32[]{:S(2)}) collective-permute-start(f32[4,16]{1,0:T(4,128)S(1)} %select_multiply_fusion.3), channel_id=1, source_target_pairs={{0,8},{8,16},{16,24},{24,32},{32,40},{40,48},{48,56},{56,64},{64,7... | collective-permute-start | bytes 776 | tf_op jit(solution)/shard_map/ppermute | solution.py:17
  26.6 6.5 %copy-start.6 = (s32[4,96]{1,0:T(4,128)S(1)}, s32[4,96]{1,0:T(4,128)}, u32[]{:S(2)}) copy-start(s32[4,96]{1,0:T(4,128)} %param.13) | copy-start | bytes 4612
  104.8 2.6 %copy-start = (f32[144,2001]{1,0:T(8,128)S(1)}, f32[144,2001]{1,0:T(8,128)}, u32[]{:S(2)}) copy-start(f32[144,2001]{1,0:T(8,128)} %get-tuple-element.23) | copy-start | bytes 3457732
  104.8 2.6 %copy-start.2 = (f32[144,2001]{1,0:T(8,128)S(1)}, f32[144,2001]{1,0:T(8,128)}, u32[]{:S(2)}) copy-start(f32[144,2001]{1,0:T(8,128)} %get-tuple-element.24) | copy-start | bytes 3457732
  107.4 1.3 %copy-start.1 = (f32[144,2001]{1,0:T(8,128)S(1)}, f32[144,2001]{1,0:T(8,128)}, u32[]{:S(2)}) copy-start(f32[144,2001]{1,0:T(8,128)} %get-tuple-element.23) | copy-start | bytes 3457732
  107.4 1.6 %copy-start.3 = (f32[144,2001]{1,0:T(8,128)S(1)}, f32[144,2001]{1,0:T(8,128)}, u32[]{:S(2)}) copy-start(f32[144,2001]{1,0:T(8,128)} %get-tuple-element.24) | copy-start | bytes 3457732
where the time goes:
time: 117 us; the launch traced here: 116 us
  blocking collectives  61 us (52%)
  other arithmetic  17.9 us (15%)
  starting transfers between devices  13.7 us (12%)
  local copies, waits for them, and re-layouts  13.6 us (12%)
  matrix products  9.57 us (8%)
    all_gather x1, blocking collectives, on_device(): lax.all_gather(local_spec, 'grp', axis=0, tiled=True)  32 us
    all_gather x1, blocking collectives, on_device(): lax.all_gather(local_mask, 'grp', axis=0, tiled=True)  29 us
    ppermute x4, starting transfers between devices, passed_along(): return lax.ppermute(array, axis, pairs)  13.7 us
    cos x1, other arithmetic, lag_basis(): return jnp.concatenate([jnp.cos(angles), -jnp.sin(angles)], axis=0)  6.09 us
    another operation x1, local copies, waits for them, and re-layouts, stacked(): jnp.stack([jnp.concatenate([right_real, right_imag], axis=1), jnp.concate...  5.52 us
    dot_general x2, matrix products, whitened(): jnp.dot(flat_traces, fourier_table(samples), precision=lax.Precision.HIGH...  4.57 us
    cos x1, other arithmetic, fourier_table(): return jnp.concatenate([jnp.cos(angles), -jnp.sin(angles)], axis=1)  3.66 us
    convert_element_type x1, other arithmetic, on_device(): return scaled.astype(jnp.bfloat16)  3.26 us
  transfers between devices with their start and end apart: 4, of which 0 were waited for; matrix products, arithmetic and copies ran while one was open for 13% of the time, Pallas kernels for 0%

commit v1 on v0

v1 whole, which is shorter than its diff:
```python
import functools
import math

import jax
import jax.numpy as jnp
import ml_dtypes
import numpy as np
from jax import lax
from jax.experimental import pallas as pl
from jax.experimental.pallas import tpu as pltpu
from jax.sharding import PartitionSpec as P

SG = 4
SEG = 16
SAMP = 1500
NBIN = 144
MAXLAG = 1000
LAGS = 2001
NGRP = 8
MAIN = 128
ROWS = SG * SEG
BLK = ROWS + 16
CHUNK = 512
BF = jnp.bfloat16
F32 = jnp.float32
MESH = pl.DeviceIdType.MESH


def split_halves(table):
    high = table.astype(ml_dtypes.bfloat16)
    low = (table - high.astype(np.float64)).astype(ml_dtypes.bfloat16)
    return high, low


def dft_table():
    n = np.arange(SAMP, dtype=np.int64)[:, None]
    k = np.arange(1, NBIN + 1, dtype=np.int64)[None, :]
    angle = ((n * k) % (2 * SAMP)).astype(np.float64) * (2.0 * np.pi / (2 * SAMP))
    taper = 0.5 - 0.5 * np.cos(2.0 * np.pi * n / SAMP)
    cos, sin = taper * np.cos(angle), -taper * np.sin(angle)
    main = np.concatenate([cos[:, :MAIN], sin[:, :MAIN]], axis=1)
    rest = np.tile(np.concatenate([cos[:, MAIN:], sin[:, MAIN:]], axis=1), (1, 4))
    main_high, main_low = split_halves(main)
    rest_high, rest_low = split_halves(rest)
    return np.concatenate([main_high, main_low, rest_high, rest_low], axis=1)


def lag_table():
    k = np.arange(1, NBIN + 1, dtype=np.int64)[:, None]
    lag = np.arange(LAGS, dtype=np.int64)[None, :] - MAXLAG
    angle = ((k * lag) % (2 * SAMP)).astype(np.float64) * (2.0 * np.pi / (2 * SAMP))
    cos = np.cos(angle) / math.sqrt(NBIN)
    sin = -np.sin(angle) / math.sqrt(NBIN)
    table = np.concatenate([cos[:MAIN], sin[:MAIN], cos[MAIN:], sin[MAIN:]], axis=0)
    return table.astype(ml_dtypes.bfloat16)


def small_tables():
    lane = np.arange(256)
    bin_of = np.where(lane < MAIN, lane + 1, MAIN + 1 + (lane - MAIN) % 16)
    counted = lane < MAIN + 32
    near = np.abs(bin_of[:, None] - bin_of[None, :]) <= 4
    weights = np.where(counted[:, None], np.where(near, 17.0, 1.0), 0.0)
    order = np.zeros((BLK, 256))
    for s in range(SG):
        for q in range(SEG):
            order[q * SG + s, s * SEG + q] = 1.0
            order[ROWS + (q % 4) * SG + s, s * SEG + q] = 1.0
    spread = np.zeros((SG * BLK, 256))
    for s in range(SG):
        for row in range(BLK):
            spread[s * BLK + row, row // SG * SG + s] = 1.0
    return np.concatenate([weights, order, spread], axis=0).astype(ml_dtypes.bfloat16)


def iota(shape, axis):
    return lax.broadcasted_iota(jnp.int32, shape, axis)


def dot(a, b):
    return jnp.dot(a, b, preferred_element_type=F32)


def lane_fold(a, shifts):
    for shift in shifts:
        a = a + pltpu.roll(a, shift, 1)
    return a


def cross_kernel(
    n_tile, x_hbm, val_hbm, rows_hbm, cnt_hbm, dft_hbm, small_hbm, f_ref,
    x_v, val_v, rows_s, cnt_s, dft_v, small_v, blk, up_down, gath, nbin, role, turned,
    out2, in2, load_sem, send_g, send_n, send_p, recv_g, recv_n, recv_p,
):
    tile, me = lax.axis_index("tile"), lax.axis_index("grp")
    z_me, y_me = me // 4, lax.rem(me, 4)
    up = lax.rem(tile + 1, n_tile)
    down = lax.rem(tile + n_tile - 1, n_tile)

    loads = [
        pltpu.make_async_copy(src, dst, load_sem.at[i])
        for i, (src, dst) in enumerate(
            [(x_hbm, x_v), (dft_hbm, dft_v), (val_hbm, val_v), (small_hbm, small_v),
             (rows_hbm, rows_s), (cnt_hbm, cnt_s)]
        )
    ]
    for load in loads:
        load.start()

    def other(d):
        return lax.rem(z_me + d // 4, 2) * 4 + lax.rem(y_me + lax.rem(d, 4), 4)

    barrier = pltpu.get_barrier_semaphore()
    for d in range(1, NGRP):
        pl.semaphore_signal(barrier, inc=1, device_id=(tile, other(d)), device_id_type=MESH)
    pl.semaphore_signal(barrier, inc=1, device_id=(up, me), device_id_type=MESH)
    pl.semaphore_signal(barrier, inc=1, device_id=(down, me), device_id_type=MESH)

    loads[2].wait()
    lane_group = iota((ROWS, 128), 1) // 32
    same_group = lane_group == (lax.rem(iota((ROWS, 128), 0), SEG) // 4)
    valid_parts = []
    for s in range(SG):
        row = jnp.broadcast_to(val_v[s : s + 1, :].astype(F32), (SEG, SEG))
        diag = jnp.where(iota((SEG, SEG), 0) == iota((SEG, SEG), 1), row, 0.0)
        valid_parts.append(jnp.sum(diag, axis=1, keepdims=True))
    valid = jnp.broadcast_to(jnp.concatenate(valid_parts, axis=0), (ROWS, 128))

    loads[0].wait()
    x = x_v[...].reshape(ROWS, SAMP)
    x_high = x.astype(BF)
    x_low = (x - x_high.astype(F32)).astype(BF)
    loads[1].wait()
    both = dot(jnp.concatenate([x_high, x_low], axis=0), dft_v[...])
    main = both[:ROWS, :256] + (both[ROWS:, :256] + both[:ROWS, 256:512])
    rest = both[:ROWS, 512:640] + (both[ROWS:, 512:640] + both[:ROWS, 640:768])
    real, imag = main[:, :MAIN], main[:, MAIN:]
    power = jnp.concatenate([real * real + imag * imag, rest * rest], axis=1)
    power_high = power.astype(BF)
    power_low = (power - power_high.astype(F32)).astype(BF)
    loads[3].wait()
    level = dot(jnp.concatenate([power_high, power_low], axis=0), small_v[0:256, :])
    level = (level[:ROWS] + level[ROWS:]) * (1.0 / 288.0) + 1e-06
    factor = lax.rsqrt(level)
    factor_main = factor[:, :MAIN] * valid
    factor_rest = jnp.where(same_group, factor[:, MAIN:] * valid, 0.0)
    white = jnp.concatenate([real * factor_main, imag * factor_main], axis=1).astype(BF)
    white_rest = jnp.concatenate(
        [rest * factor_rest, jnp.where(same_group, valid, 0.0)], axis=1
    ).astype(BF)
    blk[0:ROWS, :] = dot(small_v[256 : 256 + ROWS, 0:ROWS], white).astype(BF)
    blk[ROWS:BLK, :] = dot(small_v[256 + ROWS : 256 + BLK, 0:ROWS], white_rest).astype(BF)

    pl.semaphore_wait(barrier, NGRP + 1)

    def gather_copy(d):
        return pltpu.make_async_remote_copy(
            src_ref=blk, dst_ref=gath.at[me], send_sem=send_g.at[d - 1], recv_sem=recv_g.at[me],
            device_id=(tile, other(d)), device_id_type=MESH,
        )

    for d in range(1, NGRP):
        gather_copy(d).start()

    own = blk[...]
    gath[me] = own
    loads[4].wait()
    loads[5].wait()
    within = lax.rem(iota((BLK, BLK), 0), SG)
    same_four = (iota((BLK, BLK), 0) // SG) == (iota((BLK, BLK), 1) // SG)
    column = lax.rem(iota((BLK, BLK), 1), SG)
    neighbour = (up, down)

    def edge_copy(direction):
        return pltpu.make_async_remote_copy(
            src_ref=up_down.at[direction], dst_ref=nbin.at[direction],
            send_sem=send_n.at[direction], recv_sem=recv_n.at[direction],
            device_id=(neighbour[direction], me), device_id_type=MESH,
        )

    for direction in range(2):
        wanted = jnp.full((BLK, BLK), rows_s[0, direction, SG - 1], jnp.int32)
        for h in range(SG - 1):
            wanted = jnp.where(within == h, rows_s[0, direction, h], wanted)
        live = within < cnt_s[0, direction]
        pick = jnp.where(same_four & live & (column == wanted), 1.0, 0.0).astype(BF)
        up_down[direction] = dot(pick, own).astype(BF)
        edge_copy(direction).start()

    spread = small_v[256 + BLK : 256 + BLK + SG * BLK, 0:BLK]
    lane = iota((16, 128), 1)
    first_half = lax.rem(lane, 32) < 16

    def set_role(first, block, keep):
        wide = dot(spread, block)
        if keep is not None:
            wide = wide * keep
        for s in range(SG):
            part = wide[s * BLK : (s + 1) * BLK]
            role[first + s] = part
            tail = part[ROWS:, :128]
            turned[first + s] = jnp.where(
                first_half, pltpu.roll(tail, 112, 1), -pltpu.roll(tail, 16, 1)
            )

    set_role(0, own, None)
    for direction in range(2):
        edge_copy(direction).wait_recv()
        inside = (tile > 0) if direction == 0 else (tile < n_tile - 1)
        set_role(SG + direction * SG, nbin[direction], jnp.where(inside, 1.0, 0.0))

    sub = iota((8, 128), 0)
    low_half = sub < 4
    rest_real = lax.rem(iota((8, 128), 1), 32) < 16

    def products(j, block):
        w_re, w_im = role[j, 0:ROWS, 0:128], role[j, 0:ROWS, 128:256]
        w_rest, w_val = role[j, ROWS:BLK, 0:128], role[j, ROWS:BLK, 128:256]
        v_re, v_im = block[0:ROWS, 0:128], block[0:ROWS, 128:256]
        v_rest, v_val = block[ROWS:BLK, 0:128], block[ROWS:BLK, 128:256]
        return [
            jnp.sum(a.reshape(-1, 8, 128), axis=0)
            for a in (
                w_re * v_re + w_im * v_im,
                w_im * v_re - w_re * v_im,
                w_rest * v_rest,
                turned[j] * v_rest,
                w_val * v_val,
            )
        ]

    def finish(sums, sign):
        re, im, rest_re, rest_im, count = sums
        count = lane_fold(count, (64, 32))
        inverse = 1.0 / jnp.maximum(count, 1.0)
        rest_re = lane_fold(rest_re, (64, 32, 16))
        rest_im = lane_fold(rest_im, (64, 32, 16)) * sign
        return re * inverse, im * (inverse * sign), jnp.where(rest_real, rest_re, rest_im) * inverse

    def result_copy(d):
        return pltpu.make_async_remote_copy(
            src_ref=out2.at[d], dst_ref=in2.at[me], send_sem=send_p.at[d],
            recv_sem=recv_p.at[me], device_id=(tile, other(d)), device_id_type=MESH,
        )

    def recv_wait(buffer, sems, g):
        pltpu.make_async_copy(buffer.at[g], buffer.at[g], sems.at[g]).wait()

    def boundary(d, carry):
        g = other(d)

        @pl.when(d > 0)
        def _():
            recv_wait(gath, recv_g, g)

        block = gath[g].astype(F32)
        for pair in range(4):
            a = products(SG + 2 * pair, block)
            b = products(SG + 2 * pair + 1, block)
            both = [
                jnp.where(low_half, p, q) + pltpu.roll(jnp.where(low_half, q, p), 4, 0)
                for p, q in zip(a, b)
            ]
            done = finish(both, -1.0)
            for i in range(3):
                out2[d, 8 * pair : 8 * pair + 8, 128 * i : 128 * i + 128] = done[i].astype(BF)

        @pl.when(d > 0)
        def _():
            result_copy(d).start()

        return carry

    lax.fori_loop(0, NGRP, boundary, 0)

    def inner(d, carry):
        g = other(d)
        block = gath[g].astype(F32)
        for s in range(SG):
            sums = [a + pltpu.roll(a, 4, 0) for a in products(s, block)]
            done = finish(sums, 1.0)
            for i in range(3):
                f_ref[i, pl.ds(g * 48 + s, 4, stride=4), :] = done[i][0:4]
        return carry

    lax.fori_loop(0, NGRP, inner, 0)

    def collect(d, carry):
        g = other(d)

        @pl.when(d > 0)
        def _():
            recv_wait(in2, recv_p, g)
            start = pl.multiple_of(g * 48 + 16, 8)
            for i in range(3):
                f_ref[i, pl.ds(start, 32), :] = in2[g, :, 128 * i : 128 * i + 128].astype(F32)

        return carry

    lax.fori_loop(0, NGRP, collect, 0)
    start = pl.multiple_of(me * 48 + 16, 8)
    for i in range(3):
        f_ref[i, pl.ds(start, 32), :] = out2[0, :, 128 * i : 128 * i + 128].astype(F32)
    for d in range(1, NGRP):
        gather_copy(d).wait_send()
        result_copy(d).wait_send()
    for direction in range(2):
        edge_copy(direction).wait_send()


def lag_kernel(f_ref, mask_ref, basis_ref, out_ref, left):
    @pl.when(pl.program_id(0) == 0)
    def _():
        for s in range(SG):
            row = jnp.broadcast_to(mask_ref[s : s + 1, :].astype(F32), (96, 96))
            diag = jnp.where(iota((96, 96), 0) == iota((96, 96), 1), row, 0.0)
            keep = jnp.sum(diag, axis=1, keepdims=True)
            for i in range(3):
                rows = f_ref[i, pl.ds(s, 96, stride=4), :] * keep
                left[s * 96 : (s + 1) * 96, 128 * i : 128 * i + 128] = rows.astype(BF)

    series = dot(left[:, 0 : 2 * NBIN], basis_ref[...])
    out_ref[...] = series.reshape(SG, 96, CHUNK).astype(BF)


def on_device(n_tile, traces, validity, boundary_rows, boundary_count, pair_mask):
    dft = jnp.asarray(dft_table())
    small = jnp.asarray(small_tables())
    anywhere = pl.BlockSpec(memory_space=pltpu.MemorySpace.HBM)
    dma = pltpu.SemaphoreType.DMA
    cross = pl.pallas_call(
        functools.partial(cross_kernel, n_tile),
        out_shape=jax.ShapeDtypeStruct((3, SG * 96, 128), F32),
        in_specs=[anywhere] * 6,
        out_specs=pl.BlockSpec(memory_space=pltpu.VMEM),
        scratch_shapes=[
            pltpu.VMEM((SG, SEG, SAMP), F32),
            pltpu.VMEM((SG, SEG), jnp.int32),
            pltpu.SMEM((1, 2, SG), jnp.int32),
            pltpu.SMEM((1, 2), jnp.int32),
            pltpu.VMEM(dft.shape, BF),
            pltpu.VMEM(small.shape, BF),
            pltpu.VMEM((BLK, 256), BF),
            pltpu.VMEM((2, BLK, 256), BF),
            pltpu.VMEM((NGRP, BLK, 256), BF),
            pltpu.VMEM((2, BLK, 256), BF),
            pltpu.VMEM((12, BLK, 256), F32),
            pltpu.VMEM((12, 16, 128), F32),
            pltpu.VMEM((NGRP, 32, 384), BF),
            pltpu.VMEM((NGRP, 32, 384), BF),
            dma((6,)), dma((7,)), dma((2,)), dma((8,)), dma((8,)), dma((2,)), dma((8,)),
        ],
        compiler_params=pltpu.CompilerParams(
            collective_id=0, has_side_effects=True, vmem_limit_bytes=24 << 20
        ),
        name="cross",
    )(*[
        pltpu.with_memory_space_constraint(array, pltpu.MemorySpace.HBM)
        for array in (traces, validity, boundary_rows, boundary_count, dft, small)
    ])
    basis = jnp.asarray(lag_table())
    return pl.pallas_call(
        lag_kernel,
        out_shape=jax.ShapeDtypeStruct((SG, 96, LAGS), BF),
        grid=(pl.cdiv(LAGS, CHUNK),),
        in_specs=[
            pl.BlockSpec((3, SG * 96, 128), lambda i: (0, 0, 0)),
            pl.BlockSpec((SG, 96), lambda i: (0, 0)),
            pl.BlockSpec((2 * NBIN, CHUNK), lambda i: (0, i)),
        ],
        out_specs=pl.BlockSpec((SG, 96, CHUNK), lambda i: (0, 0, i)),
        scratch_shapes=[pltpu.VMEM((SG * 96, 384), BF)],
        compiler_params=pltpu.CompilerParams(vmem_limit_bytes=24 << 20),
        name="lags",
    )(cross, pair_mask, basis)


def solution(mesh):
    three = P(("tile", "grp"), None, None)
    two = P(("tile", "grp"), None)
    return jax.shard_map(
        functools.partial(on_device, mesh.shape["tile"]),
        mesh=mesh,
        in_specs=(three, two, three, two, two),
        out_specs=three,
        check_vma=False,
    )
```

time: 117 us -> 26.2 us (0.22)
  the two profiles are of different devices: /device:TPU:64 before, /device:TPU:32 now
where the time goes in v1:
time: 26.2 us; the launch traced here: 26.1 us
  Pallas kernels  26.1 us (100%)
    pallas_call x1, Pallas kernels, on_device(): pl.pallas_call(functools.partial(cross_kernel, n_tile), out_shape=jax.Sha...  23.3 us
    pallas_call x1, Pallas kernels, on_device(): pl.pallas_call(lag_kernel, out_shape=jax.ShapeDtypeStruct((SG, 96, LAGS),...  2.82 us

profile of v1, /device:TPU:32, one launch (start us, length us, event | category | flops | bytes accessed | tf_op | source)
XLA Modules:
  0.0 26.1 jit_solution(3340172281942597630)
XLA Ops:
  0.0 0.0 copy-start
  0.0 0.0 copy-start.1
  0.0 23.3 %cross.1.f_ref = f32[3,384,128]{2,1,0:T(8,128)S(1)} custom-call(f32[4,16,1500]{2,1,0:T(8,128)} %x_hbm.1, s32[4,16]{1,0:T(4,128)} %val_hbm.1, s32[1,2,4]{2,1,0:T(2,128)} %rows_hbm.1, s32[1,2]{1,0:T(1,128)} %cnt_hbm.1, bf16[1500,768]{1,0:T(8,128)(2,1)} %constant.6.clone.dft_hbm, bf16[656,256]{1,0:T(8,128)(2,1)} %constant.7.clone.small_hbm), custom_call_target="tpu_custom_call" | custom-call | tf_op jit(solution)/shard_map/cross/pallas_call | solution.py:331
  23.3 0.0 copy-done
  23.3 0.0 copy-done.1
  23.3 2.8 %lags.1 = bf16[4,96,2001]{2,1,0:T(8,128)(2,1)} custom-call(f32[3,384,128]{2,1,0:T(8,128)S(1)} %cross.1.f_ref, s32[4,96]{1,0:T(4,128)S(1)} %copy-done.1, bf16[288,2001]{1,0:T(8,128)(2,1)S(1)} %copy-done), custom_call_target="tpu_custom_call" | custom-call | tf_op jit(solution)/shard_map/lags/pallas_call | solution.py:362
Async XLA Ops:
  0.0 23.3 %copy-start = (bf16[288,2001]{1,0:T(8,128)(2,1)S(1)}, bf16[288,2001]{1,0:T(8,128)(2,1)}, u32[]{:S(2)}) copy-start(bf16[288,2001]{1,0:T(8,128)(2,1)} %constant.8.clone.basis_ref) | copy-start | bytes 3457732
  0.0 23.3 %copy-start.1 = (s32[4,96]{1,0:T(4,128)S(1)}, s32[4,96]{1,0:T(4,128)}, u32[]{:S(2)}) copy-start(s32[4,96]{1,0:T(4,128)} %mask_ref.1) | copy-start | bytes 4612

commit v2 on v1

--- a/solution.py
+++ b/solution.py
@@ -21,6 +21,8 @@
 ROWS = SG * SEG
 BLK = ROWS + 16
 CHUNK = 512
+DFT_PARTS = ((0, 512), (512, 1024), (1024, SAMP))
+FAR_FIRST = (6, 2, 5, 7, 1, 3, 4)
 BF = jnp.bfloat16
 F32 = jnp.float32
 MESH = pl.DeviceIdType.MESH
@@ -52,6 +54,7 @@
     cos = np.cos(angle) / math.sqrt(NBIN)
     sin = -np.sin(angle) / math.sqrt(NBIN)
     table = np.concatenate([cos[:MAIN], sin[:MAIN], cos[MAIN:], sin[MAIN:]], axis=0)
+    table = np.pad(table, ((0, 0), (0, -LAGS % CHUNK)))
     return table.astype(ml_dtypes.bfloat16)
 
 
@@ -73,6 +76,10 @@
     return np.concatenate([weights, order, spread], axis=0).astype(ml_dtypes.bfloat16)
 
 
+def arrival(step):
+    return lax.rem(step, 2) * 4 + step // 2
+
+
 def iota(shape, axis):
     return lax.broadcasted_iota(jnp.int32, shape, axis)
 
@@ -88,23 +95,31 @@
 
 
 def cross_kernel(
-    n_tile, x_hbm, val_hbm, rows_hbm, cnt_hbm, dft_hbm, small_hbm, f_ref,
-    x_v, val_v, rows_s, cnt_s, dft_v, small_v, blk, up_down, gath, nbin, role, turned,
-    out2, in2, load_sem, send_g, send_n, send_p, recv_g, recv_n, recv_p,
+    n_tile, x_hbm, val_hbm, rows_hbm, cnt_hbm, mask_hbm, dft_hbm, small_hbm, basis_hbm,
+    left_ref, basis_ref,
+    x_v, val_v, rows_s, cnt_s, mask_v, dft_v, small_v, blk, up_down, gath, nbin, role, turned,
+    keep_v, f_ref, out2, in2, load_sem, dft_sem, send_g, send_n, send_p, recv_g, recv_n, recv_p,
 ):
     tile, me = lax.axis_index("tile"), lax.axis_index("grp")
     z_me, y_me = me // 4, lax.rem(me, 4)
-    up = lax.rem(tile + 1, n_tile)
-    down = lax.rem(tile + n_tile - 1, n_tile)
+    neighbour = (tile + 1, tile - 1)
+    exists = (tile < n_tile - 1, tile > 0)
 
     loads = [
         pltpu.make_async_copy(src, dst, load_sem.at[i])
         for i, (src, dst) in enumerate(
-            [(x_hbm, x_v), (dft_hbm, dft_v), (val_hbm, val_v), (small_hbm, small_v),
-             (rows_hbm, rows_s), (cnt_hbm, cnt_s)]
+            [(x_hbm, x_v), (val_hbm, val_v), (small_hbm, small_v), (rows_hbm, rows_s),
+             (cnt_hbm, cnt_s), (mask_hbm, mask_v), (basis_hbm, basis_ref)]
         )
     ]
-    for load in loads:
+    dft_loads = [
+        pltpu.make_async_copy(dft_hbm.at[a:b], dft_v.at[a:b], dft_sem.at[i])
+        for i, (a, b) in enumerate(DFT_PARTS)
+    ]
+    loads[0].start()
+    for load in dft_loads:
+        load.start()
+    for load in loads[1:6]:
         load.start()
 
     def other(d):
@@ -113,10 +128,15 @@
     barrier = pltpu.get_barrier_semaphore()
     for d in range(1, NGRP):
         pl.semaphore_signal(barrier, inc=1, device_id=(tile, other(d)), device_id_type=MESH)
-    pl.semaphore_signal(barrier, inc=1, device_id=(up, me), device_id_type=MESH)
-    pl.semaphore_signal(barrier, inc=1, device_id=(down, me), device_id_type=MESH)
-
-    loads[2].wait()
+    for direction in range(2):
+
+        @pl.when(exists[direction])
+        def _():
+            pl.semaphore_signal(
+                barrier, inc=1, device_id=(neighbour[direction], me), device_id_type=MESH
+            )
+
+    loads[1].wait()
     lane_group = iota((ROWS, 128), 1) // 32
     same_group = lane_group == (lax.rem(iota((ROWS, 128), 0), SEG) // 4)
     valid_parts = []
@@ -130,15 +150,20 @@
     x = x_v[...].reshape(ROWS, SAMP)
     x_high = x.astype(BF)
     x_low = (x - x_high.astype(F32)).astype(BF)
-    loads[1].wait()
-    both = dot(jnp.concatenate([x_high, x_low], axis=0), dft_v[...])
+    x_both = jnp.concatenate([x_high, x_low], axis=0)
+    both = None
+    for load, (a, b) in zip(dft_loads, DFT_PARTS):
+        load.wait()
+        part = dot(x_both[:, a:b], dft_v[a:b, :])
+        both = part if both is None else both + part
+    loads[6].start()
     main = both[:ROWS, :256] + (both[ROWS:, :256] + both[:ROWS, 256:512])
     rest = both[:ROWS, 512:640] + (both[ROWS:, 512:640] + both[:ROWS, 640:768])
     real, imag = main[:, :MAIN], main[:, MAIN:]
     power = jnp.concatenate([real * real + imag * imag, rest * rest], axis=1)
     power_high = power.astype(BF)
     power_low = (power - power_high.astype(F32)).astype(BF)
-    loads[3].wait()
+    loads[2].wait()
     level = dot(jnp.concatenate([power_high, power_low], axis=0), small_v[0:256, :])
     level = (level[:ROWS] + level[ROWS:]) * (1.0 / 288.0) + 1e-06
     factor = lax.rsqrt(level)
@@ -151,7 +176,8 @@
     blk[0:ROWS, :] = dot(small_v[256 : 256 + ROWS, 0:ROWS], white).astype(BF)
     blk[ROWS:BLK, :] = dot(small_v[256 + ROWS : 256 + BLK, 0:ROWS], white_rest).astype(BF)
 
-    pl.semaphore_wait(barrier, NGRP + 1)
+    edges = jnp.where(exists[0], 1, 0) + jnp.where(exists[1], 1, 0)
+    pl.semaphore_wait(barrier, NGRP - 1 + edges)
 
     def gather_copy(d):
         return pltpu.make_async_remote_copy(
@@ -159,17 +185,16 @@
             device_id=(tile, other(d)), device_id_type=MESH,
         )
 
-    for d in range(1, NGRP):
+    for d in FAR_FIRST:
         gather_copy(d).start()
 
     own = blk[...]
     gath[me] = own
+    loads[3].wait()
     loads[4].wait()
-    loads[5].wait()
     within = lax.rem(iota((BLK, BLK), 0), SG)
     same_four = (iota((BLK, BLK), 0) // SG) == (iota((BLK, BLK), 1) // SG)
     column = lax.rem(iota((BLK, BLK), 1), SG)
-    neighbour = (up, down)
 
     def edge_copy(direction):
         return pltpu.make_async_remote_copy(
@@ -185,16 +210,17 @@
         live = within < cnt_s[0, direction]
         pick = jnp.where(same_four & live & (column == wanted), 1.0, 0.0).astype(BF)
         up_down[direction] = dot(pick, own).astype(BF)
-        edge_copy(direction).start()
+
+        @pl.when(exists[direction])
+        def _():
+            edge_copy(direction).start()
 
     spread = small_v[256 + BLK : 256 + BLK + SG * BLK, 0:BLK]
     lane = iota((16, 128), 1)
     first_half = lax.rem(lane, 32) < 16
 
-    def set_role(first, block, keep):
+    def set_role(first, block):
         wide = dot(spread, block)
-        if keep is not None:
-            wide = wide * keep
         for s in range(SG):
             part = wide[s * BLK : (s + 1) * BLK]
             role[first + s] = part
@@ -203,11 +229,27 @@
                 first_half, pltpu.roll(tail, 112, 1), -pltpu.roll(tail, 16, 1)
             )
 
-    set_role(0, own, None)
+    set_role(0, own)
+    loads[5].wait()
+    pick = (lax.rem(iota((SG * 96, 96), 0), 96) == iota((SG * 96, 96), 1)).astype(F32)
+    keep = lax.dot_general(
+        pick.astype(BF), mask_v[...].astype(F32).astype(BF), (((1,), (1,)), ((), ())),
+        preferred_element_type=F32,
+    )
+    keep = jnp.where(iota((SG * 96, SG), 0) // 96 == iota((SG * 96, SG), 1), keep, 0.0)
+    keep_v[...] = dot(keep.astype(BF), jnp.ones((SG, 128), BF))
     for direction in range(2):
-        edge_copy(direction).wait_recv()
-        inside = (tile > 0) if direction == 0 else (tile < n_tile - 1)
-        set_role(SG + direction * SG, nbin[direction], jnp.where(inside, 1.0, 0.0))
+        source = 1 - direction
+
+        @pl.when(exists[source])
+        def _():
+            edge_copy(direction).wait_recv()
+
+        @pl.when(jnp.logical_not(exists[source]))
+        def _():
+            nbin[direction] = jnp.zeros((BLK, 256), BF)
+
+        set_role(SG + direction * SG, nbin[direction])
 
     sub = iota((8, 128), 0)
     low_half = sub < 4
@@ -246,7 +288,8 @@
     def recv_wait(buffer, sems, g):
         pltpu.make_async_copy(buffer.at[g], buffer.at[g], sems.at[g]).wait()
 
-    def boundary(d, carry):
+    def boundary(step, carry):
+        d = arrival(step)
         g = other(d)
 
         @pl.when(d > 0)
@@ -305,21 +348,22 @@
         gather_copy(d).wait_send()
         result_copy(d).wait_send()
     for direction in range(2):
-        edge_copy(direction).wait_send()
-
-
-def lag_kernel(f_ref, mask_ref, basis_ref, out_ref, left):
-    @pl.when(pl.program_id(0) == 0)
-    def _():
-        for s in range(SG):
-            row = jnp.broadcast_to(mask_ref[s : s + 1, :].astype(F32), (96, 96))
-            diag = jnp.where(iota((96, 96), 0) == iota((96, 96), 1), row, 0.0)
-            keep = jnp.sum(diag, axis=1, keepdims=True)
-            for i in range(3):
-                rows = f_ref[i, pl.ds(s, 96, stride=4), :] * keep
-                left[s * 96 : (s + 1) * 96, 128 * i : 128 * i + 128] = rows.astype(BF)
-
-    series = dot(left[:, 0 : 2 * NBIN], basis_ref[...])
+
+        @pl.when(exists[direction])
+        def _():
+            edge_copy(direction).wait_send()
+
+    for s in range(SG):
+        keep = keep_v[s * 96 : (s + 1) * 96, :]
+        for i in range(3):
+            rows = f_ref[i, pl.ds(s, 96, stride=4), :] * keep
+            left_ref[s * 96 : (s + 1) * 96, 128 * i : 128 * i + 128] = rows.astype(BF)
+    loads[6].wait()
+
+
+def lag_kernel(left_ref, basis_ref, out_ref):
+    chunk = pl.ds(pl.multiple_of(pl.program_id(0) * CHUNK, CHUNK), CHUNK)
+    series = dot(left_ref[:, 0 : 2 * NBIN], basis_ref[:, chunk])
     out_ref[...] = series.reshape(SG, 96, CHUNK).astype(BF)
 
 
@@ -328,16 +372,22 @@
     small = jnp.asarray(small_tables())
     anywhere = pl.BlockSpec(memory_space=pltpu.MemorySpace.HBM)
     dma = pltpu.SemaphoreType.DMA
-    cross = pl.pallas_call(
+    vmem = pl.BlockSpec(memory_space=pltpu.VMEM)
+    basis = jnp.asarray(lag_table())
+    left, basis = pl.pallas_call(
         functools.partial(cross_kernel, n_tile),
-        out_shape=jax.ShapeDtypeStruct((3, SG * 96, 128), F32),
-        in_specs=[anywhere] * 6,
-        out_specs=pl.BlockSpec(memory_space=pltpu.VMEM),
+        out_shape=(
+            jax.ShapeDtypeStruct((SG * 96, 384), BF),
+            jax.ShapeDtypeStruct(basis.shape, BF),
+        ),
+        in_specs=[anywhere] * 8,
+        out_specs=(vmem, vmem),
         scratch_shapes=[
             pltpu.VMEM((SG, SEG, SAMP), F32),
             pltpu.VMEM((SG, SEG), jnp.int32),
             pltpu.SMEM((1, 2, SG), jnp.int32),
             pltpu.SMEM((1, 2), jnp.int32),
+            pltpu.VMEM((SG, 96), jnp.int32),
             pltpu.VMEM(dft.shape, BF),
             pltpu.VMEM(small.shape, BF),
             pltpu.VMEM((BLK, 256), BF),
@@ -346,9 +396,12 @@
             pltpu.VMEM((2, BLK, 256), BF),
             pltpu.VMEM((12, BLK, 256), F32),
             pltpu.VMEM((12, 16, 128), F32),
+            pltpu.VMEM((SG * 96, 128), F32),
+            pltpu.VMEM((3, SG * 96, 128), F32),
             pltpu.VMEM((NGRP, 32, 384), BF),
             pltpu.VMEM((NGRP, 32, 384), BF),
-            dma((6,)), dma((7,)), dma((2,)), dma((8,)), dma((8,)), dma((2,)), dma((8,)),
+            dma((7,)), dma((len(DFT_PARTS),)),
+            dma((7,)), dma((2,)), dma((8,)), dma((8,)), dma((2,)), dma((8,)),
         ],
         compiler_params=pltpu.CompilerParams(
             collective_id=0, has_side_effects=True, vmem_limit_bytes=24 << 20
@@ -356,23 +409,19 @@
         name="cross",
     )(*[
         pltpu.with_memory_space_constraint(array, pltpu.MemorySpace.HBM)
-        for array in (traces, validity, boundary_rows, boundary_count, dft, small)
+        for array in (
+            traces, validity, boundary_rows, boundary_count, pair_mask, dft, small, basis
+        )
     ])
-    basis = jnp.asarray(lag_table())
     return pl.pallas_call(
         lag_kernel,
         out_shape=jax.ShapeDtypeStruct((SG, 96, LAGS), BF),
         grid=(pl.cdiv(LAGS, CHUNK),),
-        in_specs=[
-            pl.BlockSpec((3, SG * 96, 128), lambda i: (0, 0, 0)),
-            pl.BlockSpec((SG, 96), lambda i: (0, 0)),
-            pl.BlockSpec((2 * NBIN, CHUNK), lambda i: (0, i)),
-        ],
+        in_specs=[vmem, vmem],
         out_specs=pl.BlockSpec((SG, 96, CHUNK), lambda i: (0, 0, i)),
-        scratch_shapes=[pltpu.VMEM((SG * 96, 384), BF)],
         compiler_params=pltpu.CompilerParams(vmem_limit_bytes=24 << 20),
         name="lags",
-    )(cross, pair_mask, basis)
+    )(left, basis)
 
 
 def solution(mesh):

time: 26.2 us -> 21.6 us (0.82)
  the two profiles are of different devices: /device:TPU:32 before, /device:TPU:224 now
where the time goes in v2:
time: 21.6 us; the launch traced here: 21.5 us
  Pallas kernels  21.5 us (100%)
    pallas_call x1, Pallas kernels, on_device(): pl.pallas_call(functools.partial(cross_kernel, n_tile), out_shape=(jax.Sh...  18.9 us
    pallas_call x1, Pallas kernels, on_device(): pl.pallas_call(lag_kernel, out_shape=jax.ShapeDtypeStruct((SG, 96, LAGS),...  2.62 us

profile of v2, /device:TPU:224, one launch (start us, length us, event | category | flops | bytes accessed | tf_op | source)
XLA Modules:
  0.0 21.5 jit_solution(3991482302349229733)
XLA Ops:
  0.0 18.9 %cross.1 = (bf16[384,384]{1,0:T(8,128)(2,1)S(1)}, bf16[288,2048]{1,0:T(8,128)(2,1)S(1)}) custom-call(f32[4,16,1500]{2,1,0:T(8,128)} %x_hbm.1, s32[4,16]{1,0:T(4,128)} %val_hbm.1, s32[1,2,4]{2,1,0:T(2,128)} %rows_hbm.1, s32[1,2]{1,0:T(1,128)} %cnt_hbm.1, s32[4,96]{1,0:T(4,128)} %mask_hbm.1, bf16[1500,768]{1,0:T(8,128)(2,1)} %constant.6.clone.dft_hbm, ...), custom_call_target="tpu_custom_call" | custom-call | tf_op jit(solution)/shard_map/cross/pallas_call | solution.py:377
  18.9 2.6 %lags.1 = bf16[4,96,2001]{2,1,0:T(8,128)(2,1)} custom-call(bf16[384,384]{1,0:T(8,128)(2,1)S(1)} %get-tuple-element.7.left_ref, bf16[288,2048]{1,0:T(8,128)(2,1)S(1)} %get-tuple-element.8.basis_ref), custom_call_target="tpu_custom_call" | custom-call | tf_op jit(solution)/shard_map/lags/pallas_call | solution.py:416

commit v3 on v2

v3 whole, which is shorter than its diff:
```python
import functools
import math

import jax
import jax.numpy as jnp
import ml_dtypes
import numpy as np
from jax import lax
from jax.experimental import pallas as pl
from jax.experimental.pallas import tpu as pltpu
from jax.sharding import PartitionSpec as P

SG = 4
SEG = 16
SAMP = 1500
NBIN = 144
MAXLAG = 1000
LAGS = 2001
NGRP = 8
MAIN = 128
ROWS = SG * SEG
BLK = ROWS + 16
CHUNK = 512
DFT_PARTS = ((0, 512), (512, 1024), (1024, SAMP))
BF = jnp.bfloat16
F32 = jnp.float32
MESH = pl.DeviceIdType.MESH


def split_halves(table):
    high = table.astype(ml_dtypes.bfloat16)
    low = (table - high.astype(np.float64)).astype(ml_dtypes.bfloat16)
    return high, low


def dft_table():
    n = np.arange(SAMP, dtype=np.int64)[:, None]
    k = np.arange(1, NBIN + 1, dtype=np.int64)[None, :]
    angle = ((n * k) % (2 * SAMP)).astype(np.float64) * (2.0 * np.pi / (2 * SAMP))
    taper = 0.5 - 0.5 * np.cos(2.0 * np.pi * n / SAMP)
    cos, sin = taper * np.cos(angle), -taper * np.sin(angle)
    main = np.concatenate([cos[:, :MAIN], sin[:, :MAIN]], axis=1)
    rest = np.concatenate([cos[:, MAIN:], sin[:, MAIN:]], axis=1)
    main_high, main_low = split_halves(main)
    rest_high, rest_low = split_halves(rest)
    unused = np.zeros((SAMP, 64), ml_dtypes.bfloat16)
    return np.concatenate([main_high, main_low, rest_high, rest_low, unused], axis=1)


def lag_table():
    k = np.arange(1, NBIN + 1, dtype=np.int64)[:, None]
    lag = np.arange(LAGS, dtype=np.int64)[None, :] - MAXLAG
    angle = ((k * lag) % (2 * SAMP)).astype(np.float64) * (2.0 * np.pi / (2 * SAMP))
    cos = np.cos(angle) / math.sqrt(NBIN)
    sin = -np.sin(angle) / math.sqrt(NBIN)
    table = np.concatenate([cos[:MAIN], sin[:MAIN], cos[MAIN:], sin[MAIN:]], axis=0)
    table = np.pad(table, ((0, 0), (0, -LAGS % CHUNK)))
    return table.astype(ml_dtypes.bfloat16)


def iota(shape, axis):
    return lax.broadcasted_iota(jnp.int32, shape, axis)


def dot(a, b):
    return jnp.dot(a, b, preferred_element_type=F32)


def lane_fold(a, shifts):
    for shift in shifts:
        a = a + pltpu.roll(a, shift, 1)
    return a


def bin_of(lane):
    return jnp.where(lane < MAIN, lane, MAIN + lax.rem(lane, 16))


def power_weights():
    shape = (256, 256)
    source, target = iota(shape, 0), iota(shape, 1)
    near = jnp.abs(bin_of(source) - bin_of(target)) <= 4
    return jnp.where(source < MAIN + 32, jnp.where(near, 17.0, 1.0), 0.0).astype(BF)


def cross_kernel(
    n_tile, x_hbm, val_hbm, rows_hbm, cnt_hbm, mask_hbm, dft_hbm, basis_hbm,
    left_ref, basis_ref,
    x_v, val_v, rows_s, cnt_s, mask_v, dft_v, blk, up_down, gath, nbin, role, turned,
    keep_v, f_ref, out2, in2, load_sem, dft_sem, send_g, send_n, send_p, recv_g, recv_n, recv_p,
):
    tile, me = lax.axis_index("tile"), lax.axis_index("grp")
    my_step = lax.rem(me, 4) * 2 + me // 4
    neighbour = (tile + 1, tile - 1)
    exists = (tile < n_tile - 1, tile > 0)

    def member(step):
        return lax.rem(step, 2) * 4 + step // 2

    def peer(j):
        return member(j + jnp.where(my_step <= j, 1, 0))

    loads = [
        pltpu.make_async_copy(src, dst, load_sem.at[i])
        for i, (src, dst) in enumerate(
            [(x_hbm, x_v), (val_hbm, val_v), (rows_hbm, rows_s), (cnt_hbm, cnt_s),
             (mask_hbm, mask_v), (basis_hbm, basis_ref)]
        )
    ]
    dft_loads = [
        pltpu.make_async_copy(dft_hbm.at[a:b], dft_v.at[a:b], dft_sem.at[i])
        for i, (a, b) in enumerate(DFT_PARTS)
    ]
    loads[0].start()
    loads[1].start()
    for load in dft_loads:
        load.start()
    for load in loads[2:5]:
        load.start()

    barrier = pltpu.get_barrier_semaphore()
    for j in range(NGRP - 1):
        pl.semaphore_signal(barrier, inc=1, device_id=(tile, peer(j)), device_id_type=MESH)
    for direction in range(2):

        @pl.when(exists[direction])
        def _():
            pl.semaphore_signal(
                barrier, inc=1, device_id=(neighbour[direction], me), device_id_type=MESH
            )

    row64, col64 = iota((ROWS, ROWS), 0), iota((ROWS, ROWS), 1)
    order = (col64 == lax.rem(row64, SG) * SEG + row64 // SG).astype(F32).astype(BF)
    weights = power_weights()
    loads[1].wait()
    same_group = iota((ROWS, 128), 1) // 32 == iota((ROWS, 128), 0) // 16
    lane128 = iota((ROWS, 128), 1)
    valid_parts = []
    for s in range(SG):
        row = jnp.broadcast_to(val_v[s : s + 1, :].astype(F32), (SEG, SEG))
        diag = jnp.where(iota((SEG, SEG), 0) == iota((SEG, SEG), 1), row, 0.0)
        valid_parts.append(jnp.sum(diag, axis=1, keepdims=True))
    valid = jnp.broadcast_to(jnp.concatenate(valid_parts, axis=0), (ROWS, 128))
    valid = dot(order, valid.astype(BF))
    valid_group = jnp.where(same_group, valid, 0.0)

    def stack_group(a):
        packed = (a[0:16] + a[16:32]) + (a[32:48] + a[48:64])
        return jnp.concatenate([packed[0:8], packed[8:16]], axis=1)

    loads[0].wait()
    x = x_v[...].reshape(ROWS, SAMP)
    x_high = x.astype(BF)
    x_low = (x - x_high.astype(F32)).astype(BF)
    x_both = jnp.concatenate(
        [dot(order, x_high).astype(BF), dot(order, x_low).astype(BF)], axis=0
    )
    both = None
    for load, (a, b) in zip(dft_loads, DFT_PARTS):
        load.wait()
        part = dot(x_both[:, a:b], dft_v[a:b, :])
        both = part if both is None else both + part
    loads[5].start()
    main = both[:ROWS, :256] + (both[ROWS:, :256] + both[:ROWS, 256:512])
    rest = both[:ROWS, 512:640] + jnp.where(lane128 < 32, both[ROWS:, 512:640], 0.0)
    rest = jnp.where(lane128 < 32, rest + pltpu.roll(rest, 96, 1), 0.0)
    rest = rest + pltpu.roll(rest, 32, 1)
    rest = rest + pltpu.roll(rest, 64, 1)
    real, imag = main[:, :MAIN], main[:, MAIN:]
    power = jnp.concatenate([real * real + imag * imag, rest * rest], axis=1)
    power_high = power.astype(BF)
    power_low = (power - power_high.astype(F32)).astype(BF)
    level = dot(jnp.concatenate([power_high, power_low], axis=0), weights)
    level = (level[:ROWS] + level[ROWS:]) * (1.0 / 288.0) + 1e-06
    factor = lax.rsqrt(level)
    factor_main = factor[:, :MAIN] * valid
    factor_rest = factor[:, MAIN:] * valid_group
    white = jnp.concatenate([real * factor_main, imag * factor_main], axis=1)
    own = jnp.concatenate(
        [white, stack_group(rest * factor_rest), stack_group(valid_group)], axis=0
    ).astype(BF)
    blk[...] = own

    edges = jnp.where(exists[0], 1, 0) + jnp.where(exists[1], 1, 0)
    pl.semaphore_wait(barrier, NGRP - 1 + edges)

    loads[2].wait()
    loads[3].wait()
    row, col = iota((BLK, BLK), 0), iota((BLK, BLK), 1)
    within, column = lax.rem(row, SG), lax.rem(col, SG)
    same_four = (row // SG) == (col // SG)

    def edge_copy(direction):
        return pltpu.make_async_remote_copy(
            src_ref=up_down.at[direction], dst_ref=nbin.at[direction],
            send_sem=send_n.at[direction], recv_sem=recv_n.at[direction],
            device_id=(neighbour[direction], me), device_id_type=MESH,
        )

    for direction in range(2):
        wanted = jnp.full((BLK, BLK), rows_s[0, direction, SG - 1], jnp.int32)
        for h in range(SG - 1):
            wanted = jnp.where(within == h, rows_s[0, direction, h], wanted)
        live = within < cnt_s[0, direction]
        pick = jnp.where(same_four & live & (column == wanted), 1.0, 0.0).astype(BF)
        up_down[direction] = dot(pick, own).astype(BF)

        @pl.when(exists[direction])
        def _():
            edge_copy(direction).start()

    def gather_copy(j):
        return pltpu.make_async_remote_copy(
            src_ref=blk, dst_ref=gath.at[me], send_sem=send_g.at[j], recv_sem=recv_g.at[me],
            device_id=(tile, peer(j)), device_id_type=MESH,
        )

    for j in range(NGRP - 1):
        gather_copy(j).start()
    gath[me] = own

    first_half = lax.rem(iota((8, 256), 1), 32) < 16

    def set_role(first, block):
        for s in range(SG):
            spread = (col == row // SG * SG + s).astype(F32).astype(BF)
            wide = dot(spread, block)
            role[first + s] = wide
            tail = wide[ROWS : ROWS + 8]
            ahead = jnp.concatenate(
                [pltpu.roll(tail[:, 0:128], 112, 1), pltpu.roll(tail[:, 128:], 112, 1)], axis=1
            )
            behind = jnp.concatenate(
                [pltpu.roll(tail[:, 0:128], 16, 1), pltpu.roll(tail[:, 128:], 16, 1)], axis=1
            )
            turned[first + s] = jnp.where(first_half, ahead, -behind)

    set_role(0, own)
    loads[4].wait()
    pick = (lax.rem(iota((SG * 96, 96), 0), 96) == iota((SG * 96, 96), 1)).astype(F32)
    keep = lax.dot_general(
        pick.astype(BF), mask_v[...].astype(F32).astype(BF), (((1,), (1,)), ((), ())),
        preferred_element_type=F32,
    )
    keep = jnp.where(iota((SG * 96, SG), 0) // 96 == iota((SG * 96, SG), 1), keep, 0.0)
    keep_v[...] = dot(keep.astype(BF), jnp.ones((SG, 128), BF))
    for direction in range(2):
        source = 1 - direction

        @pl.when(exists[source])
        def _():
            edge_copy(direction).wait_recv()

        @pl.when(jnp.logical_not(exists[source]))
        def _():
            nbin[direction] = jnp.zeros((BLK, 256), BF)

        set_role(SG + direction * SG, nbin[direction])

    low_half = iota((8, 128), 0) < 4
    lane = iota((8, 128), 1)
    rest_real = lax.rem(lane, 32) < 16

    def products(j, block):
        w_re, w_im = role[j, 0:ROWS, 0:128], role[j, 0:ROWS, 128:256]
        v_re, v_im = block[0:ROWS, 0:128], block[0:ROWS, 128:256]
        w_rest, v_rest = role[j, ROWS : ROWS + 8, :], block[ROWS : ROWS + 8]
        count = role[j, ROWS + 8 : BLK, :] * block[ROWS + 8 : BLK]
        rest_re = w_rest * v_rest
        rest_im = turned[j] * v_rest
        return [
            jnp.sum((w_re * v_re + w_im * v_im).reshape(-1, 8, 128), axis=0),
            jnp.sum((w_im * v_re - w_re * v_im).reshape(-1, 8, 128), axis=0),
            rest_re[:, 0:128] + rest_re[:, 128:],
            rest_im[:, 0:128] + rest_im[:, 128:],
            count[:, 0:128] + count[:, 128:],
        ]

    def finish(sums, sign):
        re, im, rest_re, rest_im, count = sums
        count = lane_fold(count, (64, 32))
        inverse = 1.0 / jnp.maximum(count, 1.0)
        rest_re = lane_fold(rest_re, (64, 32, 16))
        rest_im = lane_fold(rest_im, (64, 32, 16)) * sign
        return re * inverse, im * (inverse * sign), jnp.where(rest_real, rest_re, rest_im) * inverse

    def result_copy(g):
        return pltpu.make_async_remote_copy(
            src_ref=out2.at[g], dst_ref=in2.at[me], send_sem=send_p.at[g],
            recv_sem=recv_p.at[me], device_id=(tile, g), device_id_type=MESH,
        )

    def recv_wait(buffer, sems, g):
        pltpu.make_async_copy(buffer.at[g], buffer.at[g], sems.at[g]).wait()

    def boundary(step, carry):
        g = member(step)

        @pl.when(g != me)
        def _():
            recv_wait(gath, recv_g, g)

        block = gath[g].astype(F32)
        packed = jnp.zeros((8, 128), F32)
        for pair in range(4):
            a = products(SG + 2 * pair, block)
            b = products(SG + 2 * pair + 1, block)
            both = [
                jnp.where(low_half, p, q) + pltpu.roll(jnp.where(low_half, q, p), 4, 0)
                for p, q in zip(a, b)
            ]
            re, im, rest = finish(both, -1.0)
            out2[g, 8 * pair : 8 * pair + 8, :] = jnp.concatenate([re, im], axis=1).astype(BF)
            packed = jnp.where(lane // 32 == pair, rest, packed)
        out2[g, 32:40, :] = jnp.concatenate([packed, packed], axis=1).astype(BF)

        @pl.when(g != me)
        def _():
            result_copy(g).start()

        return carry

    lax.fori_loop(0, NGRP, boundary, 0)

    def inner(step, carry):
        g = member(step)
        block = gath[g].astype(F32)
        for s in range(SG):
            sums = [a + pltpu.roll(a, 4, 0) for a in products(s, block)]
            done = finish(sums, 1.0)
            for i in range(3):
                f_ref[i, pl.ds(g * 48 + s, 4, stride=4), :] = done[i][0:4]
        return carry

    lax.fori_loop(0, NGRP, inner, 0)

    def unpack(g, block):
        start = pl.multiple_of(g * 48 + 16, 8)
        block = block.astype(F32)
        for i in range(2):
            f_ref[i, pl.ds(start, 32), :] = block[0:32, 128 * i : 128 * i + 128]
        rest = block[32:40, 0:128]
        for pair in range(4):
            turned_rest = rest if pair == 0 else pltpu.roll(rest, 128 - 32 * pair, 1)
            f_ref[2, pl.ds(pl.multiple_of(start + 8 * pair, 8), 8), :] = turned_rest

    unpack(me, out2[me])

    def collect(step, carry):
        g = member(step)

        @pl.when(g != me)
        def _():
            recv_wait(in2, recv_p, g)
            unpack(g, in2[g])

        return carry

    lax.fori_loop(0, NGRP, collect, 0)
    for s in range(SG):
        keep = keep_v[s * 96 : (s + 1) * 96, :]
        for i in range(3):
            rows = f_ref[i, pl.ds(s, 96, stride=4), :] * keep
            left_ref[s * 96 : (s + 1) * 96, 128 * i : 128 * i + 128] = rows.astype(BF)

    for j in range(NGRP - 1):
        gather_copy(j).wait_send()
        result_copy(peer(j)).wait_send()
    for direction in range(2):

        @pl.when(exists[direction])
        def _():
            edge_copy(direction).wait_send()

    loads[5].wait()


def lag_kernel(left_ref, basis_ref, out_hbm, out_v, sems):
    copies = []
    for i, start in enumerate(range(0, LAGS, CHUNK)):
        series = dot(left_ref[:, 0 : 2 * NBIN], basis_ref[:, start : start + CHUNK])
        stop = min(start + CHUNK, LAGS)
        series = series[:, : stop - start].reshape(SG, 96, stop - start)
        out_v[:, :, start:stop] = series.astype(BF)
        copies.append(
            pltpu.make_async_copy(
                out_v.at[:, :, start:stop], out_hbm.at[:, :, start:stop], sems.at[i]
            )
        )
        copies[-1].start()
    for copy in copies:
        copy.wait()


def on_device(n_tile, traces, validity, boundary_rows, boundary_count, pair_mask):
    dft = jnp.asarray(dft_table())
    anywhere = pl.BlockSpec(memory_space=pltpu.MemorySpace.HBM)
    dma = pltpu.SemaphoreType.DMA
    vmem = pl.BlockSpec(memory_space=pltpu.VMEM)
    basis = jnp.asarray(lag_table())
    left, basis = pl.pallas_call(
        functools.partial(cross_kernel, n_tile),
        out_shape=(
            jax.ShapeDtypeStruct((SG * 96, 384), BF),
            jax.ShapeDtypeStruct(basis.shape, BF),
        ),
        in_specs=[anywhere] * 7,
        out_specs=(vmem, vmem),
        scratch_shapes=[
            pltpu.VMEM((SG, SEG, SAMP), F32),
            pltpu.VMEM((SG, SEG), jnp.int32),
            pltpu.SMEM((1, 2, SG), jnp.int32),
            pltpu.SMEM((1, 2), jnp.int32),
            pltpu.VMEM((SG, 96), jnp.int32),
            pltpu.VMEM(dft.shape, BF),
            pltpu.VMEM((BLK, 256), BF),
            pltpu.VMEM((2, BLK, 256), BF),
            pltpu.VMEM((NGRP, BLK, 256), BF),
            pltpu.VMEM((2, BLK, 256), BF),
            pltpu.VMEM((12, BLK, 256), F32),
            pltpu.VMEM((12, 8, 256), F32),
            pltpu.VMEM((SG * 96, 128), F32),
            pltpu.VMEM((3, SG * 96, 128), F32),
            pltpu.VMEM((NGRP, 40, 256), BF),
            pltpu.VMEM((NGRP, 40, 256), BF),
            dma((6,)), dma((len(DFT_PARTS),)),
            dma((7,)), dma((2,)), dma((8,)), dma((8,)), dma((2,)), dma((8,)),
        ],
        compiler_params=pltpu.CompilerParams(
            collective_id=0, has_side_effects=True, vmem_limit_bytes=24 << 20
        ),
        name="cross",
    )(*[
        pltpu.with_memory_space_constraint(array, pltpu.MemorySpace.HBM)
        for array in (
            traces, validity, boundary_rows, boundary_count, pair_mask, dft, basis
        )
    ])
    return pl.pallas_call(
        lag_kernel,
        out_shape=jax.ShapeDtypeStruct((SG, 96, LAGS), BF),
        in_specs=[vmem, vmem],
        out_specs=pl.BlockSpec(memory_space=pl.ANY),
        scratch_shapes=[
            pltpu.VMEM((SG, 96, LAGS), BF),
            pltpu.SemaphoreType.DMA((pl.cdiv(LAGS, CHUNK),)),
        ],
        compiler_params=pltpu.CompilerParams(vmem_limit_bytes=24 << 20),
        name="lags",
    )(left, basis)


def solution(mesh):
    three = P(("tile", "grp"), None, None)
    two = P(("tile", "grp"), None)
    return jax.shard_map(
        functools.partial(on_device, mesh.shape["tile"]),
        mesh=mesh,
        in_specs=(three, two, three, two, two),
        out_specs=three,
        check_vma=False,
    )
```

time: 21.6 us -> 18.4 us (0.85)
  the two profiles are of different devices: /device:TPU:224 before, /device:TPU:70 now
where the time goes in v3:
time: 18.4 us; the launch traced here: 18.3 us
  Pallas kernels  18.3 us (99%)
    pallas_call x1, Pallas kernels, on_device(): pl.pallas_call(functools.partial(cross_kernel, n_tile), out_shape=(jax.Sh...  16.5 us
    pallas_call x1, Pallas kernels, on_device(): pl.pallas_call(lag_kernel, out_shape=jax.ShapeDtypeStruct((SG, 96, LAGS),...  1.75 us

profile of v3, /device:TPU:70, one launch (start us, length us, event | category | flops | bytes accessed | tf_op | source)
XLA Modules:
  0.0 18.3 jit_solution(423944280479118225)
XLA Ops:
  0.0 16.5 %cross.1 = (bf16[384,384]{1,0:T(8,128)(2,1)S(1)}, bf16[288,2048]{1,0:T(8,128)(2,1)S(1)}) custom-call(f32[4,16,1500]{2,1,0:T(8,128)} %x_hbm.1, s32[4,16]{1,0:T(4,128)} %val_hbm.1, s32[1,2,4]{2,1,0:T(2,128)} %rows_hbm.1, s32[1,2]{1,0:T(1,128)} %cnt_hbm.1, s32[4,96]{1,0:T(4,128)} %mask_hbm.1, bf16[1500,640]{1,0:T(8,128)(2,1)} %constant.4.clone.dft_hbm, ...), custom_call_target="tpu_custom_call" | custom-call | tf_op jit(solution)/shard_map/cross/pallas_call | solution.py:401
  16.5 1.8 %lags.1 = bf16[4,96,2001]{2,1,0:T(8,128)(2,1)} custom-call(bf16[384,384]{1,0:T(8,128)(2,1)S(1)} %get-tuple-element.7.left_ref, bf16[288,2048]{1,0:T(8,128)(2,1)S(1)} %get-tuple-element.8.basis_ref), custom_call_target="tpu_custom_call" | custom-call | tf_op jit(solution)/shard_map/lags/pallas_call | solution.py:439

commit v4 on v3

--- a/solution.py
+++ b/solution.py
@@ -21,6 +21,8 @@
 ROWS = SG * SEG
 BLK = ROWS + 16
 CHUNK = 512
+X_RUN = 8
+DEAD = 15.0
 DFT_PARTS = ((0, 512), (512, 1024), (1024, SAMP))
 BF = jnp.bfloat16
 F32 = jnp.float32
@@ -86,13 +88,20 @@
 def cross_kernel(
     n_tile, x_hbm, val_hbm, rows_hbm, cnt_hbm, mask_hbm, dft_hbm, basis_hbm,
     left_ref, basis_ref,
-    x_v, val_v, rows_s, cnt_s, mask_v, dft_v, blk, up_down, gath, nbin, role, turned,
-    keep_v, f_ref, out2, in2, load_sem, dft_sem, send_g, send_n, send_p, recv_g, recv_n, recv_p,
+    x_v, val_v, rows_s, cnt_s, mask_v, dft_v, blk, gath, side, far, role, turned,
+    keep_v, code_v, f_ref, load_sem, dft_sem, send_g, send_s, send_x, send_b,
+    recv_g, recv_s, recv_x,
 ):
     tile, me = lax.axis_index("tile"), lax.axis_index("grp")
     my_step = lax.rem(me, 4) * 2 + me // 4
     neighbour = (tile + 1, tile - 1)
     exists = (tile < n_tile - 1, tile > 0)
+    core = lax.rem(tile, 2)
+    side_tile = tile + 1 - 2 * core
+    far_tile = tile - 1 + 2 * core
+    has_far = jnp.logical_and(far_tile >= 0, far_tile < n_tile)
+    turn = jnp.logical_and(has_far, (far_tile + X_RUN) // X_RUN != (tile + X_RUN) // X_RUN)
+    straight = jnp.logical_and(has_far, jnp.logical_not(turn))
 
     def member(step):
         return lax.rem(step, 2) * 4 + step // 2
@@ -143,10 +152,23 @@
     valid = jnp.broadcast_to(jnp.concatenate(valid_parts, axis=0), (ROWS, 128))
     valid = dot(order, valid.astype(BF))
     valid_group = jnp.where(same_group, valid, 0.0)
+    loads[2].wait()
+    loads[3].wait()
 
     def stack_group(a):
         packed = (a[0:16] + a[16:32]) + (a[32:48] + a[48:64])
         return jnp.concatenate([packed[0:8], packed[8:16]], axis=1)
+
+    tail = stack_group(valid_group)
+    tail_row, tail_lane = iota((8, 256), 0), iota((8, 256), 1)
+    tail = jnp.where(lax.rem(tail_lane, 32) == 31, 0.0, tail)
+    for direction in range(2):
+        for h in range(SG):
+            code = jnp.where(
+                h < cnt_s[0, direction], rows_s[0, direction, h].astype(F32), DEAD
+            )
+            here = (tail_row == h) & (tail_lane == 31 + 32 * direction)
+            tail = jnp.where(here, code, tail)
 
     loads[0].wait()
     x = x_v[...].reshape(ROWS, SAMP)
@@ -176,49 +198,40 @@
     factor_main = factor[:, :MAIN] * valid
     factor_rest = factor[:, MAIN:] * valid_group
     white = jnp.concatenate([real * factor_main, imag * factor_main], axis=1)
-    own = jnp.concatenate(
-        [white, stack_group(rest * factor_rest), stack_group(valid_group)], axis=0
-    ).astype(BF)
+    own = jnp.concatenate([white, stack_group(rest * factor_rest), tail], axis=0).astype(BF)
     blk[...] = own
+    gath[me] = own
 
     edges = jnp.where(exists[0], 1, 0) + jnp.where(exists[1], 1, 0)
     pl.semaphore_wait(barrier, NGRP - 1 + edges)
 
-    loads[2].wait()
-    loads[3].wait()
-    row, col = iota((BLK, BLK), 0), iota((BLK, BLK), 1)
-    within, column = lax.rem(row, SG), lax.rem(col, SG)
-    same_four = (row // SG) == (col // SG)
-
-    def edge_copy(direction):
+    def send(src, dst, send_sem, recv_sem, to_tile, to_member):
         return pltpu.make_async_remote_copy(
-            src_ref=up_down.at[direction], dst_ref=nbin.at[direction],
-            send_sem=send_n.at[direction], recv_sem=recv_n.at[direction],
-            device_id=(neighbour[direction], me), device_id_type=MESH,
+            src_ref=src, dst_ref=dst, send_sem=send_sem, recv_sem=recv_sem,
+            device_id=(to_tile, to_member), device_id_type=MESH,
         )
 
-    for direction in range(2):
-        wanted = jnp.full((BLK, BLK), rows_s[0, direction, SG - 1], jnp.int32)
-        for h in range(SG - 1):
-            wanted = jnp.where(within == h, rows_s[0, direction, h], wanted)
-        live = within < cnt_s[0, direction]
-        pick = jnp.where(same_four & live & (column == wanted), 1.0, 0.0).astype(BF)
-        up_down[direction] = dot(pick, own).astype(BF)
-
-        @pl.when(exists[direction])
-        def _():
-            edge_copy(direction).start()
-
     def gather_copy(j):
-        return pltpu.make_async_remote_copy(
-            src_ref=blk, dst_ref=gath.at[me], send_sem=send_g.at[j], recv_sem=recv_g.at[me],
-            device_id=(tile, peer(j)), device_id_type=MESH,
-        )
+        return send(blk, gath.at[me], send_g.at[j], recv_g.at[me], tile, peer(j))
+
+    def side_copy(g, src):
+        return send(src, side.at[g], send_s.at[g], recv_s.at[g], side_tile, me)
+
+    def far_copy(g, src):
+        return send(src, far.at[g], send_x.at[g], recv_x.at[g], far_tile, me)
+
+    def spread_copy(j):
+        return send(far.at[me], far.at[me], send_b.at[j], recv_x.at[me], tile, peer(j))
+
+    @pl.when(has_far)
+    def _():
+        far_copy(me, blk).start()
 
     for j in range(NGRP - 1):
         gather_copy(j).start()
-    gath[me] = own
-
+    side_copy(me, blk).start()
+
+    row, col = iota((BLK, BLK), 0), iota((BLK, BLK), 1)
     first_half = lax.rem(iota((8, 256), 1), 32) < 16
 
     def set_role(first, block):
@@ -237,28 +250,15 @@
 
     set_role(0, own)
     loads[4].wait()
-    pick = (lax.rem(iota((SG * 96, 96), 0), 96) == iota((SG * 96, 96), 1)).astype(F32)
-    keep = lax.dot_general(
-        pick.astype(BF), mask_v[...].astype(F32).astype(BF), (((1,), (1,)), ((), ())),
-        preferred_element_type=F32,
-    )
-    keep = jnp.where(iota((SG * 96, SG), 0) // 96 == iota((SG * 96, SG), 1), keep, 0.0)
-    keep_v[...] = dot(keep.astype(BF), jnp.ones((SG, 128), BF))
-    for direction in range(2):
-        source = 1 - direction
-
-        @pl.when(exists[source])
-        def _():
-            edge_copy(direction).wait_recv()
-
-        @pl.when(jnp.logical_not(exists[source]))
-        def _():
-            nbin[direction] = jnp.zeros((BLK, 256), BF)
-
-        set_role(SG + direction * SG, nbin[direction])
-
-    low_half = iota((8, 128), 0) < 4
+    column, line = iota((96, 96), 0), iota((96, 96), 1)
+    on_diagonal = column == line
+    for s in range(SG):
+        wanted = jnp.broadcast_to(mask_v[s : s + 1, :].astype(F32), (96, 96))
+        kept = jnp.sum(jnp.where(on_diagonal, wanted, 0.0), axis=1, keepdims=True)
+        keep_v[s] = jnp.broadcast_to(kept, (96, 128))
+
     lane = iota((8, 128), 1)
+    last_lane = lax.rem(lane, 32) == 31
     rest_real = lax.rem(lane, 32) < 16
 
     def products(j, block):
@@ -276,101 +276,109 @@
             count[:, 0:128] + count[:, 128:],
         ]
 
-    def finish(sums, sign):
+    def finish(sums):
         re, im, rest_re, rest_im, count = sums
         count = lane_fold(count, (64, 32))
+        count = jnp.where(last_lane, pltpu.roll(count, 1, 1), count)
         inverse = 1.0 / jnp.maximum(count, 1.0)
         rest_re = lane_fold(rest_re, (64, 32, 16))
-        rest_im = lane_fold(rest_im, (64, 32, 16)) * sign
-        return re * inverse, im * (inverse * sign), jnp.where(rest_real, rest_re, rest_im) * inverse
-
-    def result_copy(g):
-        return pltpu.make_async_remote_copy(
-            src_ref=out2.at[g], dst_ref=in2.at[me], send_sem=send_p.at[g],
-            recv_sem=recv_p.at[me], device_id=(tile, g), device_id_type=MESH,
-        )
+        rest_im = lane_fold(rest_im, (64, 32, 16))
+        return re * inverse, im * inverse, jnp.where(rest_real, rest_re, rest_im) * inverse
 
     def recv_wait(buffer, sems, g):
         pltpu.make_async_copy(buffer.at[g], buffer.at[g], sems.at[g]).wait()
 
-    def boundary(step, carry):
+    def columns(g, block, kind):
+        block = block.astype(F32)
+        for s in range(SG):
+            sums = [a + pltpu.roll(a, 4, 0) for a in products(s, block)]
+            done = finish(sums)
+            for i in range(3):
+                f_ref[i, pl.ds(g * 48 + kind * 16 + s, 4, stride=4), :] = done[i][0:4]
+
+    @pl.when(jnp.logical_not(has_far))
+    def _():
+        far[...] = jnp.zeros(far.shape, BF)
+
+    @pl.when(turn)
+    def _():
+        recv_wait(far, recv_x, me)
+        for j in range(NGRP - 1):
+            spread_copy(j).start()
+
+    def own_columns(step, carry):
         g = member(step)
 
         @pl.when(g != me)
         def _():
             recv_wait(gath, recv_g, g)
-
-        block = gath[g].astype(F32)
-        packed = jnp.zeros((8, 128), F32)
-        for pair in range(4):
-            a = products(SG + 2 * pair, block)
-            b = products(SG + 2 * pair + 1, block)
-            both = [
-                jnp.where(low_half, p, q) + pltpu.roll(jnp.where(low_half, q, p), 4, 0)
-                for p, q in zip(a, b)
-            ]
-            re, im, rest = finish(both, -1.0)
-            out2[g, 8 * pair : 8 * pair + 8, :] = jnp.concatenate([re, im], axis=1).astype(BF)
-            packed = jnp.where(lane // 32 == pair, rest, packed)
-        out2[g, 32:40, :] = jnp.concatenate([packed, packed], axis=1).astype(BF)
-
-        @pl.when(g != me)
+            side_copy(g, gath.at[g]).start()
+
+            @pl.when(straight)
+            def _():
+                far_copy(g, gath.at[g]).start()
+
+        columns(g, gath[g], 0)
+        return carry
+
+    lax.fori_loop(0, NGRP, own_columns, 0)
+
+    def outer_columns(step, carry):
+        g = member(step)
+        recv_wait(side, recv_s, g)
+        columns(g, side[g], 2 - core)
+
+        @pl.when(jnp.logical_or(straight, jnp.logical_and(turn, g != me)))
         def _():
-            result_copy(g).start()
-
+            recv_wait(far, recv_x, g)
+
+        columns(g, far[g], 1 + core)
         return carry
 
-    lax.fori_loop(0, NGRP, boundary, 0)
-
-    def inner(step, carry):
-        g = member(step)
-        block = gath[g].astype(F32)
-        for s in range(SG):
-            sums = [a + pltpu.roll(a, 4, 0) for a in products(s, block)]
-            done = finish(sums, 1.0)
-            for i in range(3):
-                f_ref[i, pl.ds(g * 48 + s, 4, stride=4), :] = done[i][0:4]
-        return carry
-
-    lax.fori_loop(0, NGRP, inner, 0)
-
-    def unpack(g, block):
-        start = pl.multiple_of(g * 48 + 16, 8)
-        block = block.astype(F32)
-        for i in range(2):
-            f_ref[i, pl.ds(start, 32), :] = block[0:32, 128 * i : 128 * i + 128]
-        rest = block[32:40, 0:128]
-        for pair in range(4):
-            turned_rest = rest if pair == 0 else pltpu.roll(rest, 128 - 32 * pair, 1)
-            f_ref[2, pl.ds(pl.multiple_of(start + 8 * pair, 8), 8), :] = turned_rest
-
-    unpack(me, out2[me])
-
-    def collect(step, carry):
-        g = member(step)
-
-        @pl.when(g != me)
-        def _():
-            recv_wait(in2, recv_p, g)
-            unpack(g, in2[g])
-
-        return carry
-
-    lax.fori_loop(0, NGRP, collect, 0)
+    lax.fori_loop(0, NGRP, outer_columns, 0)
+
+    def codes(buffer, g, direction):
+        rows = buffer[g, ROWS + 8 : BLK, 0:128].astype(F32)
+        picked = jnp.where(lane == 31 + 32 * direction, rows, 0.0)
+        return jnp.broadcast_to(jnp.sum(picked, axis=1, keepdims=True), (8, 128))
+
+    even = core == 0
+    for g in range(NGRP):
+        side_code = codes(side, g, 1 - core)
+        far_code = jnp.where(has_far, codes(far, g, core), DEAD)
+        code_v[g * 12 : g * 12 + 4, :] = iota((4, 128), 0).astype(F32)
+        code_v[g * 12 + 4 : g * 12 + 8, :] = jnp.where(even, far_code, side_code)[0:4]
+        code_v[g * 12 + 8 : g * 12 + 12, :] = jnp.where(even, side_code, far_code)[0:4]
+    same_list = column // SG == line // SG
+    chosen = same_list & (lax.rem(line, SG).astype(F32) == code_v[:, 0:96])
+    chosen = jnp.where(chosen, 1.0, 0.0)
     for s in range(SG):
-        keep = keep_v[s * 96 : (s + 1) * 96, :]
-        for i in range(3):
-            rows = f_ref[i, pl.ds(s, 96, stride=4), :] * keep
-            left_ref[s * 96 : (s + 1) * 96, 128 * i : 128 * i + 128] = rows.astype(BF)
+        pick = (chosen * keep_v[s][:, 0:96]).astype(BF)
+        rows = jnp.concatenate(
+            [f_ref[i, pl.ds(s, 96, stride=4), :].astype(BF) for i in range(3)], axis=1
+        )
+        left_ref[s * 96 : (s + 1) * 96, :] = dot(pick, rows).astype(BF)
 
     for j in range(NGRP - 1):
         gather_copy(j).wait_send()
-        result_copy(peer(j)).wait_send()
-    for direction in range(2):
-
-        @pl.when(exists[direction])
+    side_copy(me, blk).wait_send()
+
+    @pl.when(has_far)
+    def _():
+        far_copy(me, blk).wait_send()
+
+    @pl.when(turn)
+    def _():
+        for j in range(NGRP - 1):
+            spread_copy(j).wait_send()
+
+    for j in range(NGRP - 1):
+        g = peer(j)
+        side_copy(g, gath.at[g]).wait_send()
+
+        @pl.when(straight)
         def _():
-            edge_copy(direction).wait_send()
+            far_copy(g, gath.at[g]).wait_send()
 
     loads[5].wait()
 
@@ -414,17 +422,16 @@
             pltpu.VMEM((SG, 96), jnp.int32),
             pltpu.VMEM(dft.shape, BF),
             pltpu.VMEM((BLK, 256), BF),
-            pltpu.VMEM((2, BLK, 256), BF),
             pltpu.VMEM((NGRP, BLK, 256), BF),
-            pltpu.VMEM((2, BLK, 256), BF),
-            pltpu.VMEM((12, BLK, 256), F32),
-            pltpu.VMEM((12, 8, 256), F32),
-            pltpu.VMEM((SG * 96, 128), F32),
+            pltpu.VMEM((NGRP, BLK, 256), BF),
+            pltpu.VMEM((NGRP, BLK, 256), BF),
+            pltpu.VMEM((SG, BLK, 256), F32),
+            pltpu.VMEM((SG, 8, 256), F32),
+            pltpu.VMEM((SG, 96, 128), F32),
+            pltpu.VMEM((96, 128), F32),
             pltpu.VMEM((3, SG * 96, 128), F32),
-            pltpu.VMEM((NGRP, 40, 256), BF),
-            pltpu.VMEM((NGRP, 40, 256), BF),
             dma((6,)), dma((len(DFT_PARTS),)),
-            dma((7,)), dma((2,)), dma((8,)), dma((8,)), dma((2,)), dma((8,)),
+            dma((7,)), dma((8,)), dma((8,)), dma((7,)), dma((8,)), dma((8,)), dma((8,)),
         ],
         compiler_params=pltpu.CompilerParams(
             collective_id=0, has_side_effects=True, vmem_limit_bytes=24 << 20

time: 18.4 us -> 19.9 us (1.082)
  the two profiles are of different devices: /device:TPU:70 before, /device:TPU:95 now
where the time goes in v4:
time: 19.9 us; the launch traced here: 19.8 us
  Pallas kernels  19.8 us (99%)
    pallas_call x1, Pallas kernels, on_device(): pl.pallas_call(functools.partial(cross_kernel, n_tile), out_shape=(jax.Sh...  18.1 us
    pallas_call x1, Pallas kernels, on_device(): pl.pallas_call(lag_kernel, out_shape=jax.ShapeDtypeStruct((SG, 96, LAGS),...  1.76 us

profile of v4, /device:TPU:95, one launch (start us, length us, event | category | flops | bytes accessed | tf_op | source)
XLA Modules:
  0.0 19.8 jit_solution(17550883784109230255)
XLA Ops:
  0.0 18.1 %cross.1 = (bf16[384,384]{1,0:T(8,128)(2,1)S(1)}, bf16[288,2048]{1,0:T(8,128)(2,1)S(1)}) custom-call(f32[4,16,1500]{2,1,0:T(8,128)} %x_hbm.1, s32[4,16]{1,0:T(4,128)} %val_hbm.1, s32[1,2,4]{2,1,0:T(2,128)} %rows_hbm.1, s32[1,2]{1,0:T(1,128)} %cnt_hbm.1, s32[4,96]{1,0:T(4,128)} %mask_hbm.1, bf16[1500,640]{1,0:T(8,128)(2,1)} %constant.4.clone.dft_hbm, ...), custom_call_target="tpu_custom_call" | custom-call | tf_op jit(solution)/shard_map/cross/pallas_call | solution.py:409
  18.1 1.8 %lags.1 = bf16[4,96,2001]{2,1,0:T(8,128)(2,1)} custom-call(bf16[384,384]{1,0:T(8,128)(2,1)S(1)} %get-tuple-element.7.left_ref, bf16[288,2048]{1,0:T(8,128)(2,1)S(1)} %get-tuple-element.8.basis_ref), custom_call_target="tpu_custom_call" | custom-call | tf_op jit(solution)/shard_map/lags/pallas_call | solution.py:446

commit v5 on v4

--- a/solution.py
+++ b/solution.py
@@ -22,7 +22,7 @@
 BLK = ROWS + 16
 CHUNK = 512
 X_RUN = 8
-DEAD = 15.0
+DEAD = 128.0
 DFT_PARTS = ((0, 512), (512, 1024), (1024, SAMP))
 BF = jnp.bfloat16
 F32 = jnp.float32
@@ -89,7 +89,7 @@
     n_tile, x_hbm, val_hbm, rows_hbm, cnt_hbm, mask_hbm, dft_hbm, basis_hbm,
     left_ref, basis_ref,
     x_v, val_v, rows_s, cnt_s, mask_v, dft_v, blk, gath, side, far, role, turned,
-    keep_v, code_v, f_ref, load_sem, dft_sem, send_g, send_s, send_x, send_b,
+    keep_v, code_v, raw, f_ref, load_sem, dft_sem, send_g, send_s, send_x, send_b,
     recv_g, recv_s, recv_x,
 ):
     tile, me = lax.axis_index("tile"), lax.axis_index("grp")
@@ -259,6 +259,7 @@
 
     lane = iota((8, 128), 1)
     last_lane = lax.rem(lane, 32) == 31
+    low_half = iota((8, 128), 0) < 4
     rest_real = lax.rem(lane, 32) < 16
 
     def products(j, block):
@@ -290,11 +291,23 @@
 
     def columns(g, block, kind):
         block = block.astype(F32)
+        rows = pl.ds(pl.multiple_of(g * 8, 8), 8)
         for s in range(SG):
-            sums = [a + pltpu.roll(a, 4, 0) for a in products(s, block)]
-            done = finish(sums)
-            for i in range(3):
-                f_ref[i, pl.ds(g * 48 + kind * 16 + s, 4, stride=4), :] = done[i][0:4]
+            for i, part in enumerate(products(s, block)):
+                raw[s, kind, i, rows, :] = part
+
+    def settle(kind):
+        for s in range(SG):
+            for pair in range(NGRP // 2):
+                parts = []
+                for i in range(5):
+                    a = raw[s, kind, i, 16 * pair : 16 * pair + 8, :]
+                    b = raw[s, kind, i, 16 * pair + 8 : 16 * pair + 16, :]
+                    crossed = pltpu.roll(jnp.where(low_half, b, a), 4, 0)
+                    parts.append(jnp.where(low_half, a, b) + crossed)
+                start = kind * 32 + 8 * pair
+                for i, part in enumerate(finish(parts)):
+                    f_ref[s, start : start + 8, 128 * i : 128 * i + 128] = part
 
     @pl.when(jnp.logical_not(has_far))
     def _():
@@ -322,20 +335,28 @@
         return carry
 
     lax.fori_loop(0, NGRP, own_columns, 0)
-
-    def outer_columns(step, carry):
+    settle(0)
+
+    def side_columns(step, carry):
         g = member(step)
         recv_wait(side, recv_s, g)
-        columns(g, side[g], 2 - core)
+        columns(g, side[g], 1)
+        return carry
+
+    lax.fori_loop(0, NGRP, side_columns, 0)
+    settle(1)
+
+    def far_columns(step, carry):
+        g = member(step)
 
         @pl.when(jnp.logical_or(straight, jnp.logical_and(turn, g != me)))
         def _():
             recv_wait(far, recv_x, g)
 
-        columns(g, far[g], 1 + core)
+        columns(g, far[g], 2)
         return carry
 
-    lax.fori_loop(0, NGRP, outer_columns, 0)
+    lax.fori_loop(0, NGRP, far_columns, 0)
 
     def codes(buffer, g, direction):
         rows = buffer[g, ROWS + 8 : BLK, 0:128].astype(F32)
@@ -344,20 +365,16 @@
 
     even = core == 0
     for g in range(NGRP):
-        side_code = codes(side, g, 1 - core)
-        far_code = jnp.where(has_far, codes(far, g, core), DEAD)
-        code_v[g * 12 : g * 12 + 4, :] = iota((4, 128), 0).astype(F32)
+        side_code = codes(side, g, 1 - core) + (32.0 + 4 * g)
+        far_code = jnp.where(has_far, codes(far, g, core), DEAD) + (64.0 + 4 * g)
+        code_v[g * 12 : g * 12 + 4, :] = iota((4, 128), 0).astype(F32) + 4.0 * g
         code_v[g * 12 + 4 : g * 12 + 8, :] = jnp.where(even, far_code, side_code)[0:4]
         code_v[g * 12 + 8 : g * 12 + 12, :] = jnp.where(even, side_code, far_code)[0:4]
-    same_list = column // SG == line // SG
-    chosen = same_list & (lax.rem(line, SG).astype(F32) == code_v[:, 0:96])
-    chosen = jnp.where(chosen, 1.0, 0.0)
+    chosen = jnp.where(line.astype(F32) == code_v[:, 0:96], 1.0, 0.0)
+    settle(2)
     for s in range(SG):
         pick = (chosen * keep_v[s][:, 0:96]).astype(BF)
-        rows = jnp.concatenate(
-            [f_ref[i, pl.ds(s, 96, stride=4), :].astype(BF) for i in range(3)], axis=1
-        )
-        left_ref[s * 96 : (s + 1) * 96, :] = dot(pick, rows).astype(BF)
+        left_ref[s * 96 : (s + 1) * 96, :] = dot(pick, f_ref[s].astype(BF)).astype(BF)
 
     for j in range(NGRP - 1):
         gather_copy(j).wait_send()
@@ -429,7 +446,8 @@
             pltpu.VMEM((SG, 8, 256), F32),
             pltpu.VMEM((SG, 96, 128), F32),
             pltpu.VMEM((96, 128), F32),
-            pltpu.VMEM((3, SG * 96, 128), F32),
+            pltpu.VMEM((SG, 3, 5, 64, 128), F32),
+            pltpu.VMEM((SG, 96, 384), F32),
             dma((6,)), dma((len(DFT_PARTS),)),
             dma((7,)), dma((8,)), dma((8,)), dma((7,)), dma((8,)), dma((8,)), dma((8,)),
         ],

time: 19.9 us -> 18.8 us (0.945)
  the two profiles are of different devices: /device:TPU:95 before, /device:TPU:93 now
where the time goes in v5:
time: 18.8 us; the launch traced here: 18.7 us
  Pallas kernels  18.7 us (99%)
    pallas_call x1, Pallas kernels, on_device(): pl.pallas_call(functools.partial(cross_kernel, n_tile), out_shape=(jax.Sh...  17 us
    pallas_call x1, Pallas kernels, on_device(): pl.pallas_call(lag_kernel, out_shape=jax.ShapeDtypeStruct((SG, 96, LAGS),...  1.75 us

profile of v5, /device:TPU:93, one launch (start us, length us, event | category | flops | bytes accessed | tf_op | source)
XLA Modules:
  0.0 18.7 jit_solution(5333885533980177189)
XLA Ops:
  0.0 17.0 %cross.1 = (bf16[384,384]{1,0:T(8,128)(2,1)S(1)}, bf16[288,2048]{1,0:T(8,128)(2,1)S(1)}) custom-call(f32[4,16,1500]{2,1,0:T(8,128)} %x_hbm.1, s32[4,16]{1,0:T(4,128)} %val_hbm.1, s32[1,2,4]{2,1,0:T(2,128)} %rows_hbm.1, s32[1,2]{1,0:T(1,128)} %cnt_hbm.1, s32[4,96]{1,0:T(4,128)} %mask_hbm.1, bf16[1500,640]{1,0:T(8,128)(2,1)} %constant.4.clone.dft_hbm, ...), custom_call_target="tpu_custom_call" | custom-call | tf_op jit(solution)/shard_map/cross/pallas_call | solution.py:426
  17.0 1.8 %lags.1 = bf16[4,96,2001]{2,1,0:T(8,128)(2,1)} custom-call(bf16[384,384]{1,0:T(8,128)(2,1)S(1)} %get-tuple-element.7.left_ref, bf16[288,2048]{1,0:T(8,128)(2,1)S(1)} %get-tuple-element.8.basis_ref), custom_call_target="tpu_custom_call" | custom-call | tf_op jit(solution)/shard_map/lags/pallas_call | solution.py:464

commit v6 on v5

--- a/solution.py
+++ b/solution.py
@@ -88,9 +88,9 @@
 def cross_kernel(
     n_tile, x_hbm, val_hbm, rows_hbm, cnt_hbm, mask_hbm, dft_hbm, basis_hbm,
     left_ref, basis_ref,
-    x_v, val_v, rows_s, cnt_s, mask_v, dft_v, blk, gath, side, far, role, turned,
-    keep_v, code_v, raw, f_ref, load_sem, dft_sem, send_g, send_s, send_x, send_b,
-    recv_g, recv_s, recv_x,
+    x_v, val_v, rows_s, cnt_s, mask_v, dft_v, blk, edge, gath, side, far, nbin, role, turned,
+    keep_v, code_v, raw, f_ref, far_f, out2, in2, load_sem, dft_sem,
+    send_g, send_s, send_x, send_n, send_p, recv_g, recv_s, recv_x, recv_n, recv_p,
 ):
     tile, me = lax.axis_index("tile"), lax.axis_index("grp")
     my_step = lax.rem(me, 4) * 2 + me // 4
@@ -100,11 +100,20 @@
     side_tile = tile + 1 - 2 * core
     far_tile = tile - 1 + 2 * core
     has_far = jnp.logical_and(far_tile >= 0, far_tile < n_tile)
-    turn = jnp.logical_and(has_far, (far_tile + X_RUN) // X_RUN != (tile + X_RUN) // X_RUN)
-    straight = jnp.logical_and(has_far, jnp.logical_not(turn))
+    even = core == 0
+    odd = core == 1
+    turn = (far_tile + X_RUN) // X_RUN != (tile + X_RUN) // X_RUN
+    takes_blocks = jnp.logical_and(even, jnp.logical_and(has_far, jnp.logical_not(turn)))
+    gives_blocks = jnp.logical_and(odd, jnp.logical_and(has_far, jnp.logical_not(turn)))
+    takes_results = jnp.logical_and(has_far, jnp.logical_or(odd, turn))
+    gives_edge = jnp.logical_and(has_far, jnp.logical_or(even, turn))
 
     def member(step):
         return lax.rem(step, 2) * 4 + step // 2
+
+    def near(step):
+        d = jnp.where(step < 2, 4 * step, jnp.where(step < 6, 2 * step - 3, 4 * step - 22))
+        return lax.rem(me // 4 + d // 4, 2) * 4 + lax.rem(lax.rem(me, 4) + lax.rem(d, 4), 4)
 
     def peer(j):
         return member(j + jnp.where(my_step <= j, 1, 0))
@@ -169,6 +178,16 @@
             )
             here = (tail_row == h) & (tail_lane == 31 + 32 * direction)
             tail = jnp.where(here, code, tail)
+
+    r80, c80 = iota((BLK, BLK), 0), iota((BLK, BLK), 1)
+    within = lax.rem(r80, SG)
+    wanted = jnp.zeros((BLK, BLK), jnp.int32)
+    for h in range(SG):
+        chosen = jnp.where(even, rows_s[0, 1, h], rows_s[0, 0, h])
+        live = h < jnp.where(even, cnt_s[0, 1], cnt_s[0, 0])
+        wanted = jnp.where(within == h, jnp.where(live, chosen, SG), wanted)
+    pick_far = (r80 // SG == c80 // SG) & (lax.rem(c80, SG) == wanted)
+    pick_far = jnp.where(pick_far, 1.0, 0.0).astype(BF)
 
     loads[0].wait()
     x = x_v[...].reshape(ROWS, SAMP)
@@ -220,10 +239,20 @@
     def far_copy(g, src):
         return send(src, far.at[g], send_x.at[g], recv_x.at[g], far_tile, me)
 
-    def spread_copy(j):
-        return send(far.at[me], far.at[me], send_b.at[j], recv_x.at[me], tile, peer(j))
-
-    @pl.when(has_far)
+    def edge_copy():
+        return send(edge, nbin, send_n, recv_n, far_tile, me)
+
+    def result_copy(g):
+        return send(out2.at[g], in2.at[me], send_p.at[g], recv_p.at[me], tile, g)
+
+    row, col = iota((BLK, BLK), 0), iota((BLK, BLK), 1)
+    edge[...] = dot(pick_far, own).astype(BF)
+
+    @pl.when(gives_edge)
+    def _():
+        edge_copy().start()
+
+    @pl.when(gives_blocks)
     def _():
         far_copy(me, blk).start()
 
@@ -231,7 +260,6 @@
         gather_copy(j).start()
     side_copy(me, blk).start()
 
-    row, col = iota((BLK, BLK), 0), iota((BLK, BLK), 1)
     first_half = lax.rem(iota((8, 256), 1), 32) < 16
 
     def set_role(first, block):
@@ -277,14 +305,14 @@
             count[:, 0:128] + count[:, 128:],
         ]
 
-    def finish(sums):
+    def finish(sums, sign=1.0):
         re, im, rest_re, rest_im, count = sums
         count = lane_fold(count, (64, 32))
         count = jnp.where(last_lane, pltpu.roll(count, 1, 1), count)
         inverse = 1.0 / jnp.maximum(count, 1.0)
         rest_re = lane_fold(rest_re, (64, 32, 16))
-        rest_im = lane_fold(rest_im, (64, 32, 16))
-        return re * inverse, im * inverse, jnp.where(rest_real, rest_re, rest_im) * inverse
+        rest_im = lane_fold(rest_im, (64, 32, 16)) * sign
+        return re * inverse, im * (inverse * sign), jnp.where(rest_real, rest_re, rest_im) * inverse
 
     def recv_wait(buffer, sems, g):
         pltpu.make_async_copy(buffer.at[g], buffer.at[g], sems.at[g]).wait()
@@ -296,28 +324,38 @@
             for i, part in enumerate(products(s, block)):
                 raw[s, kind, i, rows, :] = part
 
+    def merge(first, second):
+        return [
+            jnp.where(low_half, a, b) + pltpu.roll(jnp.where(low_half, b, a), 4, 0)
+            for a, b in zip(first, second)
+        ]
+
     def settle(kind):
         for s in range(SG):
             for pair in range(NGRP // 2):
-                parts = []
-                for i in range(5):
-                    a = raw[s, kind, i, 16 * pair : 16 * pair + 8, :]
-                    b = raw[s, kind, i, 16 * pair + 8 : 16 * pair + 16, :]
-                    crossed = pltpu.roll(jnp.where(low_half, b, a), 4, 0)
-                    parts.append(jnp.where(low_half, a, b) + crossed)
+                parts = merge(
+                    [raw[s, kind, i, 16 * pair : 16 * pair + 8, :] for i in range(5)],
+                    [raw[s, kind, i, 16 * pair + 8 : 16 * pair + 16, :] for i in range(5)],
+                )
                 start = kind * 32 + 8 * pair
                 for i, part in enumerate(finish(parts)):
                     f_ref[s, start : start + 8, 128 * i : 128 * i + 128] = part
 
-    @pl.when(jnp.logical_not(has_far))
-    def _():
-        far[...] = jnp.zeros(far.shape, BF)
-
-    @pl.when(turn)
-    def _():
-        recv_wait(far, recv_x, me)
-        for j in range(NGRP - 1):
-            spread_copy(j).start()
+    @pl.when(takes_results)
+    def _():
+        edge_copy().wait_recv()
+        set_role(SG, nbin[...])
+
+    def results(g):
+        block = gath[g].astype(F32)
+        packed = jnp.zeros((8, 128), F32)
+        for pair in range(2):
+            re, im, rest = finish(
+                merge(products(SG + 2 * pair, block), products(SG + 2 * pair + 1, block)), -1.0
+            )
+            out2[g, 8 * pair : 8 * pair + 8, :] = jnp.concatenate([re, im], axis=1).astype(BF)
+            packed = jnp.where(lane // 32 == pair, rest, packed)
+        out2[g, 16:24, :] = jnp.concatenate([packed, packed], axis=1).astype(BF)
 
     def own_columns(step, carry):
         g = member(step)
@@ -327,9 +365,17 @@
             recv_wait(gath, recv_g, g)
             side_copy(g, gath.at[g]).start()
 
-            @pl.when(straight)
+            @pl.when(gives_blocks)
             def _():
                 far_copy(g, gath.at[g]).start()
+
+        @pl.when(takes_results)
+        def _():
+            results(g)
+
+            @pl.when(g != me)
+            def _():
+                result_copy(g).start()
 
         columns(g, gath[g], 0)
         return carry
@@ -346,56 +392,90 @@
     lax.fori_loop(0, NGRP, side_columns, 0)
     settle(1)
 
-    def far_columns(step, carry):
-        g = member(step)
-
-        @pl.when(jnp.logical_or(straight, jnp.logical_and(turn, g != me)))
-        def _():
-            recv_wait(far, recv_x, g)
-
-        columns(g, far[g], 2)
-        return carry
-
-    lax.fori_loop(0, NGRP, far_columns, 0)
+    def unpack(g, block):
+        rows = block.astype(F32)
+        start = pl.multiple_of(g * 16, 8)
+        for i in range(2):
+            far_f[i, pl.ds(start, 16), :] = rows[0:16, 128 * i : 128 * i + 128]
+        rest = rows[16:24, 0:128]
+        far_f[2, pl.ds(start, 8), :] = rest
+        far_f[2, pl.ds(pl.multiple_of(start + 8, 8), 8), :] = pltpu.roll(rest, 96, 1)
 
     def codes(buffer, g, direction):
         rows = buffer[g, ROWS + 8 : BLK, 0:128].astype(F32)
         picked = jnp.where(lane == 31 + 32 * direction, rows, 0.0)
         return jnp.broadcast_to(jnp.sum(picked, axis=1, keepdims=True), (8, 128))
 
-    even = core == 0
+    @pl.when(takes_results)
+    def _():
+        unpack(me, out2[me])
+
+        def collect(step, carry):
+            g = member(step)
+
+            @pl.when(g != me)
+            def _():
+                recv_wait(in2, recv_p, g)
+                unpack(g, in2[g])
+
+            return carry
+
+        lax.fori_loop(0, NGRP, collect, 0)
+        for s in range(SG):
+            for i in range(3):
+                outer = far_f[i, pl.ds(s, 32, stride=4), :]
+                f_ref[s, 64:96, 128 * i : 128 * i + 128] = outer
+
+    @pl.when(takes_blocks)
+    def _():
+        def far_columns(step, carry):
+            g = member(step)
+            recv_wait(far, recv_x, g)
+            columns(g, far[g], 2)
+            return carry
+
+        lax.fori_loop(0, NGRP, far_columns, 0)
+        settle(2)
+
+    @pl.when(jnp.logical_not(has_far))
+    def _():
+        f_ref[:, 64:96, :] = jnp.zeros((SG, 32, 384), F32)
+
     for g in range(NGRP):
         side_code = codes(side, g, 1 - core) + (32.0 + 4 * g)
-        far_code = jnp.where(has_far, codes(far, g, core), DEAD) + (64.0 + 4 * g)
+        far_code = jnp.where(takes_blocks, codes(far, g, core), iota((8, 128), 0).astype(F32))
+        far_code = far_code + (64.0 + 4 * g)
         code_v[g * 12 : g * 12 + 4, :] = iota((4, 128), 0).astype(F32) + 4.0 * g
         code_v[g * 12 + 4 : g * 12 + 8, :] = jnp.where(even, far_code, side_code)[0:4]
         code_v[g * 12 + 8 : g * 12 + 12, :] = jnp.where(even, side_code, far_code)[0:4]
     chosen = jnp.where(line.astype(F32) == code_v[:, 0:96], 1.0, 0.0)
-    settle(2)
     for s in range(SG):
         pick = (chosen * keep_v[s][:, 0:96]).astype(BF)
-        left_ref[s * 96 : (s + 1) * 96, :] = dot(pick, f_ref[s].astype(BF)).astype(BF)
-
-    for j in range(NGRP - 1):
-        gather_copy(j).wait_send()
+        rows = f_ref[s].astype(BF)
+        left_ref[s * 96 : (s + 1) * 96, :] = dot(pick, rows).astype(BF)
+
     side_copy(me, blk).wait_send()
 
-    @pl.when(has_far)
+    @pl.when(gives_edge)
+    def _():
+        edge_copy().wait_send()
+
+    @pl.when(gives_blocks)
     def _():
         far_copy(me, blk).wait_send()
-
-    @pl.when(turn)
-    def _():
-        for j in range(NGRP - 1):
-            spread_copy(j).wait_send()
 
     for j in range(NGRP - 1):
         g = peer(j)
+        gather_copy(j).wait_send()
         side_copy(g, gath.at[g]).wait_send()
 
-        @pl.when(straight)
+        @pl.when(gives_blocks)
         def _():
             far_copy(g, gath.at[g]).wait_send()
+
+        @pl.when(takes_results)
+        def _():
+            result_copy(g).wait_send()
 
     loads[5].wait()
 
@@ -439,17 +519,23 @@
             pltpu.VMEM((SG, 96), jnp.int32),
             pltpu.VMEM(dft.shape, BF),
             pltpu.VMEM((BLK, 256), BF),
+            pltpu.VMEM((BLK, 256), BF),
             pltpu.VMEM((NGRP, BLK, 256), BF),
             pltpu.VMEM((NGRP, BLK, 256), BF),
             pltpu.VMEM((NGRP, BLK, 256), BF),
-            pltpu.VMEM((SG, BLK, 256), F32),
-            pltpu.VMEM((SG, 8, 256), F32),
+            pltpu.VMEM((BLK, 256), BF),
+            pltpu.VMEM((2 * SG, BLK, 256), F32),
+            pltpu.VMEM((2 * SG, 8, 256), F32),
             pltpu.VMEM((SG, 96, 128), F32),
             pltpu.VMEM((96, 128), F32),
             pltpu.VMEM((SG, 3, 5, 64, 128), F32),
             pltpu.VMEM((SG, 96, 384), F32),
+            pltpu.VMEM((3, 128, 128), F32),
+            pltpu.VMEM((NGRP, 24, 256), BF),
+            pltpu.VMEM((NGRP, 24, 256), BF),
             dma((6,)), dma((len(DFT_PARTS),)),
-            dma((7,)), dma((8,)), dma((8,)), dma((7,)), dma((8,)), dma((8,)), dma((8,)),
+            dma((7,)), dma((8,)), dma((8,)), dma(()), dma((8,)),
+            dma((8,)), dma((8,)), dma((8,)), dma(()), dma((8,)),
         ],
         compiler_params=pltpu.CompilerParams(
             collective_id=0, has_side_effects=True, vmem_limit_bytes=24 << 20

time: 18.8 us -> 18.1 us (0.963)
  the two profiles are of different devices: /device:TPU:93 before, /device:TPU:64 now
where the time goes in v6:
time: 18.1 us; the launch traced here: 17.8 us
  Pallas kernels  17.8 us (98%)
    pallas_call x1, Pallas kernels, on_device(): pl.pallas_call(functools.partial(cross_kernel, n_tile), out_shape=(jax.Sh...  16.1 us
    pallas_call x1, Pallas kernels, on_device(): pl.pallas_call(lag_kernel, out_shape=jax.ShapeDtypeStruct((SG, 96, LAGS),...  1.75 us

profile of v6, /device:TPU:64, one launch (start us, length us, event | category | flops | bytes accessed | tf_op | source)
XLA Modules:
  0.0 17.8 jit_solution(5058410452962735804)
XLA Ops:
  0.0 16.1 %cross.1 = (bf16[384,384]{1,0:T(8,128)(2,1)S(1)}, bf16[288,2048]{1,0:T(8,128)(2,1)S(1)}) custom-call(f32[4,16,1500]{2,1,0:T(8,128)} %x_hbm.1, s32[4,16]{1,0:T(4,128)} %val_hbm.1, s32[1,2,4]{2,1,0:T(2,128)} %rows_hbm.1, s32[1,2]{1,0:T(1,128)} %cnt_hbm.1, s32[4,96]{1,0:T(4,128)} %mask_hbm.1, bf16[1500,640]{1,0:T(8,128)(2,1)} %constant.4.clone.dft_hbm, ...), custom_call_target="tpu_custom_call" | custom-call | tf_op jit(solution)/shard_map/cross/pallas_call | solution.py:506
  16.1 1.8 %lags.1 = bf16[4,96,2001]{2,1,0:T(8,128)(2,1)} custom-call(bf16[384,384]{1,0:T(8,128)(2,1)S(1)} %get-tuple-element.7.left_ref, bf16[288,2048]{1,0:T(8,128)(2,1)S(1)} %get-tuple-element.8.basis_ref), custom_call_target="tpu_custom_call" | custom-call | tf_op jit(solution)/shard_map/lags/pallas_call | solution.py:550

commit v7 on v6

--- a/solution.py
+++ b/solution.py
@@ -22,8 +22,8 @@
 BLK = ROWS + 16
 CHUNK = 512
 X_RUN = 8
+DFT_PARTS = tuple((a, min(a + 768, SAMP)) for a in range(0, SAMP, 768))
 DEAD = 128.0
-DFT_PARTS = ((0, 512), (512, 1024), (1024, SAMP))
 BF = jnp.bfloat16
 F32 = jnp.float32
 MESH = pl.DeviceIdType.MESH
@@ -75,7 +75,7 @@
 
 
 def bin_of(lane):
-    return jnp.where(lane < MAIN, lane, MAIN + lax.rem(lane, 16))
+    return jnp.where(lane < MAIN, lane, MAIN + (lane & 15))
 
 
 def power_weights():
@@ -129,11 +129,10 @@
         pltpu.make_async_copy(dft_hbm.at[a:b], dft_v.at[a:b], dft_sem.at[i])
         for i, (a, b) in enumerate(DFT_PARTS)
     ]
+    for load in loads[1:5]:
+        load.start()
     loads[0].start()
-    loads[1].start()
     for load in dft_loads:
-        load.start()
-    for load in loads[2:5]:
         load.start()
 
     barrier = pltpu.get_barrier_semaphore()
@@ -147,11 +146,16 @@
                 barrier, inc=1, device_id=(neighbour[direction], me), device_id_type=MESH
             )
 
-    row64, col64 = iota((ROWS, ROWS), 0), iota((ROWS, ROWS), 1)
-    order = (col64 == lax.rem(row64, SG) * SEG + row64 // SG).astype(F32).astype(BF)
+    row80, col64 = iota((BLK, ROWS), 0), iota((BLK, ROWS), 1)
+    head = row80 < ROWS
+    same_station = (row80 & 3) == (col64 >> 4)
+    segment = col64 & 15
+    source = jnp.where(head, row80 >> 2, (row80 - ROWS) >> 2)
+    order = same_station & (jnp.where(head, segment, segment & 3) == source)
+    order = order.astype(F32).astype(BF)
     weights = power_weights()
     loads[1].wait()
-    same_group = iota((ROWS, 128), 1) // 32 == iota((ROWS, 128), 0) // 16
+    same_group = (iota((ROWS, 128), 1) >> 5) == ((iota((ROWS, 128), 0) & 15) >> 2)
     lane128 = iota((ROWS, 128), 1)
     valid_parts = []
     for s in range(SG):
@@ -159,18 +163,16 @@
         diag = jnp.where(iota((SEG, SEG), 0) == iota((SEG, SEG), 1), row, 0.0)
         valid_parts.append(jnp.sum(diag, axis=1, keepdims=True))
     valid = jnp.broadcast_to(jnp.concatenate(valid_parts, axis=0), (ROWS, 128))
-    valid = dot(order, valid.astype(BF))
     valid_group = jnp.where(same_group, valid, 0.0)
     loads[2].wait()
     loads[3].wait()
 
-    def stack_group(a):
-        packed = (a[0:16] + a[16:32]) + (a[32:48] + a[48:64])
-        return jnp.concatenate([packed[0:8], packed[8:16]], axis=1)
-
-    tail = stack_group(valid_group)
+    def fold_rows(a):
+        return jnp.concatenate([a[0:8], a[8:16]], axis=1)
+
+    tail = fold_rows(dot(order[ROWS:], valid_group.astype(BF)))
     tail_row, tail_lane = iota((8, 256), 0), iota((8, 256), 1)
-    tail = jnp.where(lax.rem(tail_lane, 32) == 31, 0.0, tail)
+    tail = jnp.where((tail_lane & 31) == 31, 0.0, tail)
     for direction in range(2):
         for h in range(SG):
             code = jnp.where(
@@ -180,27 +182,23 @@
             tail = jnp.where(here, code, tail)
 
     r80, c80 = iota((BLK, BLK), 0), iota((BLK, BLK), 1)
-    within = lax.rem(r80, SG)
+    within = r80 & 3
     wanted = jnp.zeros((BLK, BLK), jnp.int32)
     for h in range(SG):
         chosen = jnp.where(even, rows_s[0, 1, h], rows_s[0, 0, h])
         live = h < jnp.where(even, cnt_s[0, 1], cnt_s[0, 0])
         wanted = jnp.where(within == h, jnp.where(live, chosen, SG), wanted)
-    pick_far = (r80 // SG == c80 // SG) & (lax.rem(c80, SG) == wanted)
+    pick_far = ((r80 >> 2) == (c80 >> 2)) & ((c80 & 3) == wanted)
     pick_far = jnp.where(pick_far, 1.0, 0.0).astype(BF)
 
     loads[0].wait()
     x = x_v[...].reshape(ROWS, SAMP)
     x_high = x.astype(BF)
     x_low = (x - x_high.astype(F32)).astype(BF)
-    x_both = jnp.concatenate(
-        [dot(order, x_high).astype(BF), dot(order, x_low).astype(BF)], axis=0
-    )
-    both = None
-    for load, (a, b) in zip(dft_loads, DFT_PARTS):
+    x_both = jnp.concatenate([x_high, x_low], axis=0)
+    for load in dft_loads:
         load.wait()
-        part = dot(x_both[:, a:b], dft_v[a:b, :])
-        both = part if both is None else both + part
+    both = dot(x_both, dft_v[...])
     loads[5].start()
     main = both[:ROWS, :256] + (both[ROWS:, :256] + both[:ROWS, 256:512])
     rest = both[:ROWS, 512:640] + jnp.where(lane128 < 32, both[ROWS:, 512:640], 0.0)
@@ -217,7 +215,9 @@
     factor_main = factor[:, :MAIN] * valid
     factor_rest = factor[:, MAIN:] * valid_group
     white = jnp.concatenate([real * factor_main, imag * factor_main], axis=1)
-    own = jnp.concatenate([white, stack_group(rest * factor_rest), tail], axis=0).astype(BF)
+    white = dot(order[:ROWS], white.astype(BF))
+    white_rest = fold_rows(dot(order[ROWS:], (rest * factor_rest).astype(BF)))
+    own = jnp.concatenate([white, white_rest, tail], axis=0).astype(BF)
     blk[...] = own
     gath[me] = own
 
@@ -245,11 +245,11 @@
     def result_copy(g):
         return send(out2.at[g], in2.at[me], send_p.at[g], recv_p.at[me], tile, g)
 
-    row, col = iota((BLK, BLK), 0), iota((BLK, BLK), 1)
-    edge[...] = dot(pick_far, own).astype(BF)
-
-    @pl.when(gives_edge)
-    def _():
+    on_turn = jnp.logical_and(has_far, turn)
+
+    @pl.when(on_turn)
+    def _():
+        edge[...] = dot(pick_far, own).astype(BF)
         edge_copy().start()
 
     @pl.when(gives_blocks)
@@ -258,13 +258,19 @@
 
     for j in range(NGRP - 1):
         gather_copy(j).start()
+
+    @pl.when(jnp.logical_and(gives_edge, jnp.logical_not(turn)))
+    def _():
+        edge[...] = dot(pick_far, own).astype(BF)
+        edge_copy().start()
+
     side_copy(me, blk).start()
-
-    first_half = lax.rem(iota((8, 256), 1), 32) < 16
+    row, col = iota((BLK, BLK), 0), iota((BLK, BLK), 1)
+    first_half = (iota((8, 256), 1) & 31) < 16
 
     def set_role(first, block):
         for s in range(SG):
-            spread = (col == row // SG * SG + s).astype(F32).astype(BF)
+            spread = (col == (row >> 2) * SG + s).astype(F32).astype(BF)
             wide = dot(spread, block)
             role[first + s] = wide
             tail = wide[ROWS : ROWS + 8]
@@ -286,9 +292,9 @@
         keep_v[s] = jnp.broadcast_to(kept, (96, 128))
 
     lane = iota((8, 128), 1)
-    last_lane = lax.rem(lane, 32) == 31
+    last_lane = (lane & 31) == 31
     low_half = iota((8, 128), 0) < 4
-    rest_real = lax.rem(lane, 32) < 16
+    rest_real = (lane & 31) < 16
 
     def products(j, block):
         w_re, w_im = role[j, 0:ROWS, 0:128], role[j, 0:ROWS, 128:256]
@@ -354,7 +360,7 @@
                 merge(products(SG + 2 * pair, block), products(SG + 2 * pair + 1, block)), -1.0
             )
             out2[g, 8 * pair : 8 * pair + 8, :] = jnp.concatenate([re, im], axis=1).astype(BF)
-            packed = jnp.where(lane // 32 == pair, rest, packed)
+            packed = jnp.where((lane >> 5) == pair, rest, packed)
         out2[g, 16:24, :] = jnp.concatenate([packed, packed], axis=1).astype(BF)
 
     def own_columns(step, carry):
@@ -394,21 +400,31 @@
 
     def unpack(g, block):
         rows = block.astype(F32)
-        start = pl.multiple_of(g * 16, 8)
+        start = g * 16
         for i in range(2):
             far_f[i, pl.ds(start, 16), :] = rows[0:16, 128 * i : 128 * i + 128]
         rest = rows[16:24, 0:128]
         far_f[2, pl.ds(start, 8), :] = rest
-        far_f[2, pl.ds(pl.multiple_of(start + 8, 8), 8), :] = pltpu.roll(rest, 96, 1)
+        far_f[2, pl.ds(start + 8, 8), :] = pltpu.roll(rest, 96, 1)
 
     def codes(buffer, g, direction):
         rows = buffer[g, ROWS + 8 : BLK, 0:128].astype(F32)
         picked = jnp.where(lane == 31 + 32 * direction, rows, 0.0)
         return jnp.broadcast_to(jnp.sum(picked, axis=1, keepdims=True), (8, 128))
 
+    station = iota((8, 128), 0).astype(F32)
+
+    def place(g, first, second):
+        code_v[g * 12 + 4 : g * 12 + 8, :] = jnp.where(even, first, second)[0:4]
+        code_v[g * 12 + 8 : g * 12 + 12, :] = jnp.where(even, second, first)[0:4]
+
+    for g in range(NGRP):
+        code_v[g * 12 : g * 12 + 4, :] = station[0:4] + 4.0 * g
+        place(g, station + (64.0 + 4 * g), codes(side, g, 1 - core) + (32.0 + 4 * g))
+
     @pl.when(takes_results)
     def _():
-        unpack(me, out2[me])
+        in2[me] = out2[me]
 
         def collect(step, carry):
             g = member(step)
@@ -416,11 +432,12 @@
             @pl.when(g != me)
             def _():
                 recv_wait(in2, recv_p, g)
-                unpack(g, in2[g])
 
             return carry
 
         lax.fori_loop(0, NGRP, collect, 0)
+        for g in range(NGRP):
+            unpack(g, in2[g])
         for s in range(SG):
             for i in range(3):
                 outer = far_f[i, pl.ds(s, 32, stride=4), :]
@@ -435,19 +452,15 @@
             return carry
 
         lax.fori_loop(0, NGRP, far_columns, 0)
+        for g in range(NGRP):
+            far_code = codes(far, g, 0) + (64.0 + 4 * g)
+            code_v[g * 12 + 4 : g * 12 + 8, :] = far_code[0:4]
         settle(2)
 
     @pl.when(jnp.logical_not(has_far))
     def _():
         f_ref[:, 64:96, :] = jnp.zeros((SG, 32, 384), F32)
 
-    for g in range(NGRP):
-        side_code = codes(side, g, 1 - core) + (32.0 + 4 * g)
-        far_code = jnp.where(takes_blocks, codes(far, g, core), iota((8, 128), 0).astype(F32))
-        far_code = far_code + (64.0 + 4 * g)
-        code_v[g * 12 : g * 12 + 4, :] = iota((4, 128), 0).astype(F32) + 4.0 * g
-        code_v[g * 12 + 4 : g * 12 + 8, :] = jnp.where(even, far_code, side_code)[0:4]
-        code_v[g * 12 + 8 : g * 12 + 12, :] = jnp.where(even, side_code, far_code)[0:4]
     chosen = jnp.where(line.astype(F32) == code_v[:, 0:96], 1.0, 0.0)
     for s in range(SG):
         pick = (chosen * keep_v[s][:, 0:96]).astype(BF)

time: 18.1 us -> 17.9 us (0.989)
  Pallas kernels: 17.8 us -> 17.6 us
    pallas_call x1, Pallas kernels: 16.1 us -> 15.8 us  [on_device(): pl.pallas_call(functools.partial(cross_kernel, n_tile), out_shape=(jax.Sh...]
where the time goes in v7:
time: 17.9 us; the launch traced here: 17.6 us
  Pallas kernels  17.6 us (98%)
    pallas_call x1, Pallas kernels, on_device(): pl.pallas_call(functools.partial(cross_kernel, n_tile), out_shape=(jax.Sh...  15.8 us
    pallas_call x1, Pallas kernels, on_device(): pl.pallas_call(lag_kernel, out_shape=jax.ShapeDtypeStruct((SG, 96, LAGS),...  1.76 us

profile of v7, /device:TPU:64, one launch (start us, length us, event | category | flops | bytes accessed | tf_op | source)
XLA Modules:
  0.0 17.6 jit_solution(12262373597352213477)
XLA Ops:
  0.0 15.8 %cross.1 = (bf16[384,384]{1,0:T(8,128)(2,1)S(1)}, bf16[288,2048]{1,0:T(8,128)(2,1)S(1)}) custom-call(f32[4,16,1500]{2,1,0:T(8,128)} %x_hbm.1, s32[4,16]{1,0:T(4,128)} %val_hbm.1, s32[1,2,4]{2,1,0:T(2,128)} %rows_hbm.1, s32[1,2]{1,0:T(1,128)} %cnt_hbm.1, s32[4,96]{1,0:T(4,128)} %mask_hbm.1, bf16[1500,640]{1,0:T(8,128)(2,1)} %constant.4.clone.dft_hbm, ...), custom_call_target="tpu_custom_call" | custom-call | tf_op jit(solution)/shard_map/cross/pallas_call | solution.py:519
  15.8 1.8 %lags.1 = bf16[4,96,2001]{2,1,0:T(8,128)(2,1)} custom-call(bf16[384,384]{1,0:T(8,128)(2,1)S(1)} %get-tuple-element.7.left_ref, bf16[288,2048]{1,0:T(8,128)(2,1)S(1)} %get-tuple-element.8.basis_ref), custom_call_target="tpu_custom_call" | custom-call | tf_op jit(solution)/shard_map/lags/pallas_call | solution.py:563

commit v8 on v7

--- a/solution.py
+++ b/solution.py
@@ -352,41 +352,50 @@
         edge_copy().wait_recv()
         set_role(SG, nbin[...])
 
-    def results(g):
-        block = gath[g].astype(F32)
-        packed = jnp.zeros((8, 128), F32)
-        for pair in range(2):
-            re, im, rest = finish(
-                merge(products(SG + 2 * pair, block), products(SG + 2 * pair + 1, block)), -1.0
-            )
-            out2[g, 8 * pair : 8 * pair + 8, :] = jnp.concatenate([re, im], axis=1).astype(BF)
-            packed = jnp.where((lane >> 5) == pair, rest, packed)
-        out2[g, 16:24, :] = jnp.concatenate([packed, packed], axis=1).astype(BF)
+    def results(members):
+        done = []
+        for g in members:
+            block = gath[g].astype(F32)
+            done.append([
+                finish(
+                    merge(products(SG + 2 * pair, block), products(SG + 2 * pair + 1, block)),
+                    -1.0,
+                )
+                for pair in range(2)
+            ])
+        for g, pairs in zip(members, done):
+            for pair, (re, im, rest) in enumerate(pairs):
+                out2[g, 8 * pair : 8 * pair + 8, :] = jnp.concatenate([re, im], axis=1).astype(BF)
+            packed = jnp.where((lane >> 5) == 0, pairs[0][2], pairs[1][2])
+            out2[g, 16:24, :] = jnp.concatenate([packed, packed], axis=1).astype(BF)
 
     def own_columns(step, carry):
-        g = member(step)
-
-        @pl.when(g != me)
-        def _():
-            recv_wait(gath, recv_g, g)
-            side_copy(g, gath.at[g]).start()
-
-            @pl.when(gives_blocks)
+        members = (step, step + 4)
+        for g in members:
+
+            @pl.when(g != me)
             def _():
-                far_copy(g, gath.at[g]).start()
+                recv_wait(gath, recv_g, g)
+                side_copy(g, gath.at[g]).start()
+
+                @pl.when(gives_blocks)
+                def _():
+                    far_copy(g, gath.at[g]).start()
 
         @pl.when(takes_results)
         def _():
-            results(g)
-
-            @pl.when(g != me)
-            def _():
-                result_copy(g).start()
-
-        columns(g, gath[g], 0)
+            results(members)
+            for g in members:
+
+                @pl.when(g != me)
+                def _():
+                    result_copy(g).start()
+
+        for g in members:
+            columns(g, gath[g], 0)
         return carry
 
-    lax.fori_loop(0, NGRP, own_columns, 0)
+    lax.fori_loop(0, NGRP // 2, own_columns, 0)
     settle(0)
 
     def side_columns(step, carry):

time: 17.9 us -> 17.9 us (level)
  no operation moved by 1% of the time
where the time goes in v8:
time: 17.9 us; the launch traced here: 17.6 us
  Pallas kernels  17.6 us (98%)
    pallas_call x1, Pallas kernels, on_device(): pl.pallas_call(functools.partial(cross_kernel, n_tile), out_shape=(jax.Sh...  15.8 us
    pallas_call x1, Pallas kernels, on_device(): pl.pallas_call(lag_kernel, out_shape=jax.ShapeDtypeStruct((SG, 96, LAGS),...  1.76 us

profile of v8, /device:TPU:64, one launch (start us, length us, event | category | flops | bytes accessed | tf_op | source)
XLA Modules:
  0.0 17.6 jit_solution(6441896626202854947)
XLA Ops:
  0.0 15.8 %cross.1 = (bf16[384,384]{1,0:T(8,128)(2,1)S(1)}, bf16[288,2048]{1,0:T(8,128)(2,1)S(1)}) custom-call(f32[4,16,1500]{2,1,0:T(8,128)} %x_hbm.1, s32[4,16]{1,0:T(4,128)} %val_hbm.1, s32[1,2,4]{2,1,0:T(2,128)} %rows_hbm.1, s32[1,2]{1,0:T(1,128)} %cnt_hbm.1, s32[4,96]{1,0:T(4,128)} %mask_hbm.1, bf16[1500,640]{1,0:T(8,128)(2,1)} %constant.4.clone.dft_hbm, ...), custom_call_target="tpu_custom_call" | custom-call | tf_op jit(solution)/shard_map/cross/pallas_call | solution.py:528
  15.8 1.8 %lags.1 = bf16[4,96,2001]{2,1,0:T(8,128)(2,1)} custom-call(bf16[384,384]{1,0:T(8,128)(2,1)S(1)} %get-tuple-element.7.left_ref, bf16[288,2048]{1,0:T(8,128)(2,1)S(1)} %get-tuple-element.8.basis_ref), custom_call_target="tpu_custom_call" | custom-call | tf_op jit(solution)/shard_map/lags/pallas_call | solution.py:572

commit v9 on v7

--- a/solution.py
+++ b/solution.py
@@ -247,7 +247,7 @@
 
     on_turn = jnp.logical_and(has_far, turn)
 
-    @pl.when(on_turn)
+    @pl.when(gives_edge)
     def _():
         edge[...] = dot(pick_far, own).astype(BF)
         edge_copy().start()
@@ -258,11 +258,6 @@
 
     for j in range(NGRP - 1):
         gather_copy(j).start()
-
-    @pl.when(jnp.logical_and(gives_edge, jnp.logical_not(turn)))
-    def _():
-        edge[...] = dot(pick_far, own).astype(BF)
-        edge_copy().start()
 
     side_copy(me, blk).start()
     row, col = iota((BLK, BLK), 0), iota((BLK, BLK), 1)

time: 17.9 us -> 17.7 us (0.989); the launches traced: 17.6 us -> 17.6 us
  no operation moved by 1% of the time
where the time goes in v9:
time: 17.7 us; the launch traced here: 17.6 us
  Pallas kernels  17.6 us (99%)
    pallas_call x1, Pallas kernels, on_device(): pl.pallas_call(functools.partial(cross_kernel, n_tile), out_shape=(jax.Sh...  15.8 us
    pallas_call x1, Pallas kernels, on_device(): pl.pallas_call(lag_kernel, out_shape=jax.ShapeDtypeStruct((SG, 96, LAGS),...  1.76 us

profile of v9, /device:TPU:64, one launch (start us, length us, event | category | flops | bytes accessed | tf_op | source)
XLA Modules:
  0.0 17.6 jit_solution(6269570589846887514)
XLA Ops:
  0.0 15.8 %cross.1 = (bf16[384,384]{1,0:T(8,128)(2,1)S(1)}, bf16[288,2048]{1,0:T(8,128)(2,1)S(1)}) custom-call(f32[4,16,1500]{2,1,0:T(8,128)} %x_hbm.1, s32[4,16]{1,0:T(4,128)} %val_hbm.1, s32[1,2,4]{2,1,0:T(2,128)} %rows_hbm.1, s32[1,2]{1,0:T(1,128)} %cnt_hbm.1, s32[4,96]{1,0:T(4,128)} %mask_hbm.1, bf16[1500,640]{1,0:T(8,128)(2,1)} %constant.4.clone.dft_hbm, ...), custom_call_target="tpu_custom_call" | custom-call | tf_op jit(solution)/shard_map/cross/pallas_call | solution.py:514
  15.8 1.8 %lags.1 = bf16[4,96,2001]{2,1,0:T(8,128)(2,1)} custom-call(bf16[384,384]{1,0:T(8,128)(2,1)S(1)} %get-tuple-element.7.left_ref, bf16[288,2048]{1,0:T(8,128)(2,1)S(1)} %get-tuple-element.8.basis_ref), custom_call_target="tpu_custom_call" | custom-call | tf_op jit(solution)/shard_map/lags/pallas_call | solution.py:558
